TPU v7x, 256 devices: a whole 4x4x8 slice. The times are simulated.
256 devices in a mesh: gx: 32 (over y, x, core), gy: 8 (over z).
Axes of the slice: x: 4, y: 4, z: 8, core: 2. Of those that a mesh axis runs over, the one named last changes fastest.
Arguments:
- displacement: float32 [3, 32, 256, 1024], P(None, None, 'gx', 'gy'), may hold values from -6 to 6
- velocity: float32 [3, 32, 256, 1024], P(None, None, 'gx', 'gy'), may hold values from -6 to 6
- slopes: float32 [2, 32, 256, 1024], P(None, None, 'gx', 'gy'), may hold values from -0.5 to 0.5
- stretch: float32 [32, 256, 1024], P(None, 'gx', 'gy'), may hold values from 0.6 to 1.4
- moduli: float32 [2, 32, 256, 1024], P(None, None, 'gx', 'gy'), may hold values from 0.3 to 1
- buoyancy: float32 [32, 256, 1024], P(None, 'gx', 'gy'), may hold values from 0.5 to 1.5
- probes: float32 [4, 512, 128], P(None, 'gy'), may hold values from -0.0017089844 to 0.0017089844
Outputs:
- final_displacement: float32 [3, 32, 256, 1024], P(None, None, 'gx', 'gy')
- basis: float32 [128, 48, 128], P('gx', 'gy')
- factor: float32 [128, 128], replicated
All inputs are finite; a program needn't handle non-finite values.
Results may differ from a plain program's by a relative error of at most 0.0003.
Values sent between devices are 32-bit elements; how exact they have to be, the bound alone decides.
A program may use at most 64 MiB of HBM per device.

v0:
```python
import math

import jax
import jax.numpy as jnp
from jax import lax
from jax.sharding import PartitionSpec as P

STEPS = 4


time_step = 0.12


def extended(block, sides, width):
    for axis, dim in sides:
        count = lax.axis_size(axis)
        forward = [(i, i + 1) for i in range(count - 1)]
        backward = [(target, source) for source, target in forward]
        low = lax.ppermute(
            lax.slice_in_dim(block, block.shape[dim] - width, None, axis=dim), axis, forward
        )
        high = lax.ppermute(lax.slice_in_dim(block, 0, width, axis=dim), axis, backward)
        block = jnp.concatenate([low, block, high], axis=dim)
    return block


def fourth(values, dimension):
    length_out = values.shape[dimension] - 4

    def segment(offset):
        return lax.slice_in_dim(values, offset, offset + length_out, axis=dimension)

    return (segment(0) - segment(4) + 8.0 * (segment(3) - segment(1))) / 12.0


def vertical(values):
    padded = jnp.pad(values, ((0, 0), (2, 2), (0, 0), (0, 0)))
    return fourth(padded, 1)


def gradient(padded, slope_x, slope_y, stretch):
    d_x = fourth(padded[:, :, :, 2:-2], 2)
    d_y = fourth(padded[:, :, 2:-2, :], 3)
    d_r = vertical(padded[:, :, 2:-2, 2:-2])
    return jnp.stack([d_x + slope_x * d_r, d_y + slope_y * d_r, stretch * d_r], axis=1)


def stresses(gradients, lame, shear):
    divergence = gradients[0, 0] + gradients[1, 1] + gradients[2, 2]
    pressure = lame * divergence
    return jnp.stack(
        [
            pressure + 2.0 * shear * gradients[0, 0],
            pressure + 2.0 * shear * gradients[1, 1],
            pressure + 2.0 * shear * gradients[2, 2],
            shear * (gradients[0, 1] + gradients[1, 0]),
            shear * (gradients[0, 2] + gradients[2, 0]),
            shear * (gradients[1, 2] + gradients[2, 1]),
        ]
    )


def forces(padded, slope_x, slope_y, stretch):
    d_x = fourth(padded[:, :, :, 2:-2], 2)
    d_y = fourth(padded[:, :, 2:-2, :], 3)
    d_r = vertical(padded[:, :, 2:-2, 2:-2])
    rows_x = (0, 3, 4)
    rows_y = (3, 1, 5)
    rows_z = (4, 5, 2)
    return jnp.stack(
        [
            d_x[rows_x[component]]
            + slope_x * d_r[rows_x[component]]
            + d_y[rows_y[component]]
            + slope_y * d_r[rows_y[component]]
            + stretch * d_r[rows_z[component]]
            for component in range(3)
        ]
    )


def lower_factor(gram):
    order = gram.shape[0]
    positions = jnp.arange(order, dtype=jnp.int32)

    def column_step(column_index, lower):
        picker = (positions == column_index).astype(jnp.float32)
        column = jnp.dot(gram, picker, precision=lax.Precision.HIGHEST)
        row_of = jnp.dot(picker, lower, precision=lax.Precision.HIGHEST)
        column = column - jnp.dot(lower, row_of, precision=lax.Precision.HIGHEST)
        pivot = jnp.sqrt(jnp.sum(column * picker))
        entries = jnp.where(
            positions > column_index,
            column / pivot,
            jnp.where(positions == column_index, pivot, 0.0),
        )
        return lower + entries[:, None] * picker[None, :]

    return lax.fori_loop(0, order, column_step, jnp.zeros_like(gram))


def lower_inverse(lower):
    order = lower.shape[0]
    positions = jnp.arange(order, dtype=jnp.int32)

    def row_step(row_index, inverse):
        picker = (positions == row_index).astype(jnp.float32)
        row_of = jnp.dot(picker, lower, precision=lax.Precision.HIGHEST)
        pivot = jnp.sum(row_of * picker)
        fresh = (picker - jnp.dot(row_of, inverse, precision=lax.Precision.HIGHEST)) / pivot
        return inverse + picker[:, None] * fresh[None, :]

    return lax.fori_loop(0, order, row_step, jnp.zeros_like(lower))


def orthogonalize(tall_block, gram):
    lower = lower_factor(gram)
    inverse = lower_inverse(lower)
    result = jnp.dot(
        tall_block, inverse.T, precision=lax.Precision.HIGHEST, preferred_element_type=jnp.float32
    )
    return (result, lower.T)


def shards(displacement, velocity, slopes, stretch, moduli, buoyancy, probes):
    previous = displacement - time_step * velocity
    current = displacement
    for moment in range(STEPS):
        padded = extended(current, (("gx", 2), ("gy", 3)), 2)
        gradients = gradient(padded, slopes[0], slopes[1], stretch)
        stress = extended(stresses(gradients, moduli[0], moduli[1]), (("gx", 2), ("gy", 3)), 2)
        pushes = buoyancy * forces(stress, slopes[0], slopes[1], stretch)
        following = 2.0 * current - previous + time_step**2 * pushes
        velocities = (following - previous) / (2.0 * time_step)
        sampled = velocities[:, ::2, ::2, ::2]
        half_x = sampled.shape[2]
        rearranged = jnp.transpose(sampled, (2, 0, 1, 3)).reshape(-1, sampled.shape[3])
        sketch_term = jnp.dot(
            rearranged,
            probes[moment],
            precision=lax.Precision.HIGHEST,
            preferred_element_type=jnp.float32,
        ).reshape(half_x, -1, probes.shape[2])
        reduced = lax.psum_scatter(sketch_term, "gy", scatter_dimension=1, tiled=True)
        sketch = reduced if moment == 0 else sketch + reduced
        previous, current = (current, following)
    tall_block = sketch.reshape(-1, sketch.shape[2])
    rows_total = tall_block.shape[0] * lax.axis_size("gx") * lax.axis_size("gy")
    gram_local = jnp.dot(
        tall_block.T,
        tall_block,
        precision=lax.Precision.HIGHEST,
        preferred_element_type=jnp.float32,
    )
    gram_whole = lax.psum(gram_local, ("gx", "gy"))
    orthonormal, factor = orthogonalize(tall_block, gram_whole)
    basis = (math.sqrt(rows_total) * orthonormal).reshape(sketch.shape)
    return (current, basis, factor)


def solution(mesh):
    in_specs = (
        P(None, None, "gx", "gy"),
        P(None, None, "gx", "gy"),
        P(None, None, "gx", "gy"),
        P(None, "gx", "gy"),
        P(None, None, "gx", "gy"),
        P(None, "gx", "gy"),
        P(None, "gy", None),
    )
    out_specs = (P(None, None, "gx", "gy"), P("gx", "gy", None), P())
    return jax.shard_map(shards, mesh=mesh, in_specs=in_specs, out_specs=out_specs, check_vma=False)
```

profile of v0, /device:TPU:1, one launch (start us, length us, event | category | flops | bytes accessed | tf_op | source)
XLA Modules:
  0.0 1194.3 jit_solution(5939340690643367252)
XLA Ops:
  8.8 4.6 collective-permute-start
  18.1 4.4 collective-permute-done.1
  26.6 4.9 collective-permute-start.2
  35.1 3.8 fusion.119
  49.6 4.4 collective-permute-done.5
  59.1 3.6 collective-permute-start.6
  76.9 3.5 collective-permute-start.8
  82.4 4.0 collective-permute-done.9
  89.0 3.7 collective-permute-start.10
  107.4 4.4 collective-permute-done.13
  117.2 5.1 collective-permute-start.14
  141.4 6.0 slice.1072
  150.9 3.6 collective-permute-start.18
  163.3 5.1 collective-permute-start.20
  171.9 6.0 slice.1074
  185.3 3.9 collective-permute-start.22
  202.2 5.1 collective-permute-start.24
  225.0 5.1 collective-permute-start.28
  233.0 4.0 collective-permute-done.29
  243.1 3.7 collective-permute-start.30
  266.5 78.0 %all-reduce.14.cloned.1.call-done = f32[4,48,128]{2,0,1:T(4,128)} async-done(((f32[4,48,128]{2,0,1:T(4,128)}), f32[4,48,128]{2,0,1:T(4,128)}) %all-reduce.14.cloned.1.call-update) | async-done | bytes 98320
  347.2 245.3 %all-reduce.12.cloned.1.call-done = f32[128,128]{1,0:T(8,128)} async-done(((f32[128,128]{1,0:T(8,128)}), f32[128,128]{1,0:T(8,128)}) %all-reduce.12.cloned.1.call-update) | async-done | bytes 65552 | tf_op jit(solution)/shard_map/psum | solution.py:155
  592.5 363.3 %while.30 = (s32[]{:T(128)}, f32[128,128]{1,0:T(8,128)S(1)}, f32[128,128]{1,0:T(8,128)}, s32[]{:T(128)}, s32[]{:T(128)}) while((s32[]{:T(128)}, f32[128,128]{1,0:T(8,128)S(1)}, f32[128,128]{1,0:T(8,128)}, s32[]{:T(128)}, s32[]{:T(128)}) %tuple.125), condition=%wide.region_7.8_spmd.clone.clone, body=%wide.region_5.7_spmd.clone.clone.sunk | while | flops 673410 | bytes 332917 | solution.py:99
  956.5 230.0 %while.29 = (s32[]{:T(128)}, f32[128,128]{1,0:T(8,128)S(1)}, f32[128,128]{1,0:T(8,128)S(1)}, s32[]{:T(128)}, s32[]{:T(128)}) while((s32[]{:T(128)}, f32[128,128]{1,0:T(8,128)S(1)}, f32[128,128]{1,0:T(8,128)S(1)}, s32[]{:T(128)}, s32[]{:T(128)}) %tuple.128), condition=%wide.region_10.11_spmd.clone, body=%wide.region_8.10_spmd.clone.sunk | while | flops 460034 | bytes 265316 | solution.py:113
  (1549 shorter events, 667.7 us)
Async XLA Ops:
  7.2 337.4 %all-reduce.14.cloned.1.call-start = ((), (), s32[]{:S(2)}) async-start(), calls=%async_computation.1 | async-start | bytes 196608
  8.8 9.3 collective-permute-start
  13.4 9.1 collective-permute-start.1
  25.3 16.2 %collective-permute-start.3 = (f32[3,32,12,2]{1,3,2,0:T(2,128)}, f32[3,32,12,2]{1,3,2,0:T(2,128)}, u32[]{:S(2)}, u32[]{:S(2)}) collective-permute-start(f32[3,32,12,2]{1,3,2,0:T(2,128)} %get-tuple-element.276), channel_id=1, source_target_pairs={{1,0},{2,1},{3,2},{4,3},{5,4},{6,5},{7,6},{9,8},{10,9},{11,10},{12... | collective-permute-start | bytes 27656 | tf_op jit(solution)/shard_map/ppermute | solution.py:22
  26.6 13.8 %collective-permute-start.2 = (f32[3,32,12,2]{1,3,2,0:T(2,128)}, f32[3,32,12,2]{1,3,2,0:T(2,128)}, u32[]{:S(2)}, u32[]{:S(2)}) collective-permute-start(f32[3,32,12,2]{1,3,2,0:T(2,128)} %get-tuple-element.277), channel_id=1, source_target_pairs={{0,1},{1,2},{2,3},{3,4},{4,5},{5,6},{6,7},{8,9},{9,10},{10,11},{11... | collective-permute-start | bytes 27656 | tf_op jit(solution)/shard_map/ppermute | solution.py:19
  47.0 7.0 collective-permute-start.5
  59.1 10.4 collective-permute-start.6
  80.4 5.9 collective-permute-start.9
  89.0 9.1 collective-permute-start.10
  104.8 7.0 collective-permute-start.13
  117.2 13.2 %collective-permute-start.14 = (f32[6,32,12,2]{1,3,2,0:T(2,128)S(1)}, f32[6,32,12,2]{1,3,2,0:T(2,128)S(1)}, u32[]{:S(2)}, u32[]{:S(2)}) collective-permute-start(f32[6,32,12,2]{1,3,2,0:T(2,128)S(1)} %copy.329), channel_id=1, source_target_pairs={{0,1},{1,2},{2,3},{3,4},{4,5},{5,6},{6,7},{8,9},{9,10},{10,11},{11... | collective-permute-start | bytes 55304 | tf_op jit(solution)/shard_map/ppermute | solution.py:19
  136.6 11.5 collective-permute-start.16
  139.5 8.6 collective-permute-start.17
  150.9 8.8 collective-permute-start.18
  163.3 15.3 %collective-permute-start.20 = (f32[6,32,2,128]{3,1,2,0:T(8,128)S(1)}, f32[6,32,2,128]{3,1,2,0:T(8,128)S(1)}, u32[]{:S(2)}, u32[]{:S(2)}) collective-permute-start(f32[6,32,2,128]{3,1,2,0:T(8,128)S(1)} %get-tuple-element.294), channel_id=1, source_target_pairs={{0,8},{8,16},{16,24},{24,32},{32,40},{40,48},{48,56},{56,64},{64,7... | collective-permute-start | bytes 589832 | tf_op jit(solution)/shard_map/ppermute | solution.py:19
  168.4 10.2 collective-permute-start.21
  185.3 11.0 collective-permute-start.22
  202.2 11.8 collective-permute-start.24
  207.3 6.7 collective-permute-start.25
  214.9 7.5 collective-permute-start.26
  225.0 8.0 collective-permute-start.28
  230.1 7.0 collective-permute-start.29
  243.1 11.6 collective-permute-start.30
  265.2 327.3 %all-reduce.12.cloned.1.call-start = ((), (), s32[]{:S(2)}) async-start(), calls=%async_computation | async-start | bytes 131072 | tf_op jit(solution)/shard_map/psum | solution.py:155
  (52 other events, 254.3 us)
Sparse Core Ops, SparseCore 0:
  265.3 79.1 all-reduce.13
  351.5 240.9 all-reduce.11
where the time goes:
time: 1210 us; the launch traced here: 1190 us
  matrix products  475 us (39%)
  waiting for transfers between devices  362 us (30%)
  loops' own time  98.3 us (8%)
  starting transfers between devices  89 us (7%)
  local copies, waits for them, and re-layouts  85.4 us (7%)
  other arithmetic  68.3 us (6%)
  between operations  15.9 us (1%)
    psum x1, waiting for transfers between devices, shards(): gram_whole = lax.psum(gram_local, ('gx', 'gy'))  245 us
    dot_general x128, matrix products, column_step(): column = jnp.dot(gram, picker, precision=lax.Precision.HIGHEST)  124 us
    dot_general x128, matrix products, column_step(): column = column - jnp.dot(lower, row_of, precision=lax.Precision.HIGHEST)  108 us
    dot_general x128, matrix products, row_step(): jnp.dot(row_of, inverse, precision=lax.Precision.HIGHEST)  107 us
    dot_general x128, matrix products, row_step(): row_of = jnp.dot(picker, lower, precision=lax.Precision.HIGHEST)  105 us
    another operation x1, loops' own time, lower_factor(): return lax.fori_loop(0, order, column_step, jnp.zeros_like(gram))  94 us
    unnamed x3, waiting for transfers between devices  78.1 us
    ppermute x16, starting transfers between devices, extended(): lax.ppermute(lax.slice_in_dim(block, block.shape[dim] - width, None, axis...  62.5 us
  transfers between devices with their start and end apart: 34, of which 17 were waited for; matrix products, arithmetic and copies ran while one was open for 5% of the time, Pallas kernels for 0%

commit v1 on v0

v1 whole, which is shorter than its diff:
```python
import functools
import math

import jax
import jax.numpy as jnp
from jax import lax
from jax.experimental import pallas as pl
from jax.experimental.pallas import tpu as pltpu
from jax.sharding import PartitionSpec as P

STEPS = 4
DT = 0.12
MESH = pl.DeviceIdType.MESH
HIGH = lax.Precision.HIGHEST
F32 = jnp.float32
ZP = 48
VMEM = pltpu.MemorySpace.VMEM


def lanes():
    return lax.broadcasted_iota(jnp.int32, (8, 128), 1)


def shifted(f, h, lane):
    m2 = pltpu.roll(jnp.where(lane >= 126, h, f), 2, 1)
    m1 = pltpu.roll(jnp.where(lane >= 127, h, f), 1, 1)
    p1 = pltpu.roll(jnp.where(lane < 1, h, f), 127, 1)
    p2 = pltpu.roll(jnp.where(lane < 2, h, f), 126, 1)
    return m2, m1, p1, p2


def combine(m2, m1, p1, p2):
    return (m2 - p2) + 8.0 * (p1 - m1)


def wave_kernel(
    disp, vel, slopes, stretch, moduli, buoy, probes,
    out, pieces,
    U, S, MET, RATE, PE, SK, PU, PS, HU, HS,
    send_u, recv_u, send_s, recv_s,
):
    gx, gy = lax.axis_index("gx"), lax.axis_index("gy")
    nx, ny = lax.axis_size("gx"), lax.axis_size("gy")
    left = (lax.rem(gx + nx - 1, nx), gy)
    right = (lax.rem(gx + 1, nx), gy)
    down = (gx, lax.rem(gy + ny - 1, ny))
    up = (gx, lax.rem(gy + 1, ny))
    barrier = pltpu.get_barrier_semaphore()
    for peer in (left, right, down, up):
        pl.semaphore_signal(barrier, inc=1, device_id=peer, device_id_type=MESH)

    lane = lanes()
    zero8 = jnp.zeros((8, 128), F32)

    @pl.loop(0, 12)
    def _(x):
        for s in range(2):
            for c in range(3):
                U[s, c, x, 0:8, :] = zero8
                U[s, c, x, 40:48, :] = zero8
        for c in range(6):
            S[c, x, 0:8, :] = zero8
            S[c, x, 40:48, :] = zero8

    for n in range(STEPS):
        PE[n] = jnp.zeros((128, 128), F32)
        PE[n, pl.ds(0, 64, stride=2), :] = probes[n] * (1.0 / (2.0 * DT))
    SK[...] = jnp.zeros_like(SK)

    def load(x, carry):
        packed = list(carry)
        for zb in range(4):
            rows = pl.ds(zb * 64 + x, 8, stride=8)
            zs = slice(zb * 8, zb * 8 + 8)
            zu = slice(zb * 8 + 8, zb * 8 + 16)
            MET[0, x, zs, :] = slopes[0, rows, :]
            MET[1, x, zs, :] = slopes[1, rows, :]
            MET[2, x, zs, :] = stretch[rows, :]
            MET[3, x, zs, :] = moduli[0, rows, :] * (1.0 / 12.0)
            MET[4, x, zs, :] = moduli[1, rows, :] * (1.0 / 12.0)
            MET[5, x, zs, :] = buoy[rows, :] * (DT * DT / 12.0)
            k = x * 4 + zb
            for c in range(3):
                d = disp[c, rows, :]
                U[0, c, x + 2, zu, :] = d
                U[1, c, x + 2, zu, :] = d - DT * vel[c, rows, :]
                packed[c] = jnp.where((lane >> 2) == k, pltpu.roll(d, 4 * k + 2, 1), packed[c])
        return tuple(packed)

    packed = lax.fori_loop(0, 8, load, (zero8,) * 3)
    pl.semaphore_wait(barrier, 4)

    def exchange(planes, halo_lo, halo_hi, own_lo, own_hi, packed_ref, halo_ref, send, recv):
        copies = [
            pltpu.make_async_remote_copy(
                src_ref=planes(own_lo), dst_ref=planes(halo_hi), send_sem=send.at[0], recv_sem=recv.at[0],
                device_id=left, device_id_type=MESH),
            pltpu.make_async_remote_copy(
                src_ref=planes(own_hi), dst_ref=planes(halo_lo), send_sem=send.at[1], recv_sem=recv.at[1],
                device_id=right, device_id_type=MESH),
            pltpu.make_async_remote_copy(
                src_ref=packed_ref, dst_ref=halo_ref.at[1], send_sem=send.at[2], recv_sem=recv.at[2],
                device_id=down, device_id_type=MESH),
            pltpu.make_async_remote_copy(
                src_ref=packed_ref, dst_ref=halo_ref.at[0], send_sem=send.at[3], recv_sem=recv.at[3],
                device_id=up, device_id_type=MESH),
        ]
        for copy in copies:
            copy.start()
        return copies

    low_part = (lane & 3) < 2

    def halo_of(halo_ref, c):
        lo = jnp.where(gy == 0, zero8, halo_ref[0, c])
        hi = jnp.where(gy == ny - 1, zero8, halo_ref[1, c])
        return jnp.where(low_part, lo, hi)

    def clear(planes_at):
        zeros = jnp.zeros((3, 2, 32, 128), F32)

        @pl.when(gx == 0)
        def _():
            planes_at(slice(0, 2))[...] = zeros

        @pl.when(gx == nx - 1)
        def _():
            planes_at(slice(10, 12))[...] = zeros

    for c in range(3):
        PU[c] = packed[c]

    def step(n, carry):
        cur = lax.rem(n, 2)
        old = 1 - cur

        def u_planes(xs):
            return U.at[cur, :, xs, 8:40, :]

        def s_planes(xs):
            return S.at[0:3, xs, 8:40, :]

        copies = exchange(u_planes, slice(0, 2), slice(10, 12), slice(2, 4), slice(8, 10), PU, HU, send_u, recv_u)

        @pl.when(n > 0)
        def _():
            sketch(n - 1)

        for copy in copies:
            copy.wait()
        clear(u_planes)
        halos = [halo_of(HU, c) for c in range(3)]

        def stress(x, packed):
            packed = list(packed)
            for zb in range(4):
                z0 = zb * 8
                zs = slice(z0, z0 + 8)
                zu = slice(z0 + 8, z0 + 16)
                k = x * 4 + zb
                sx, sy, st = MET[0, x, zs, :], MET[1, x, zs, :], MET[2, x, zs, :]
                lam, mu = MET[3, x, zs, :], MET[4, x, zs, :]
                g = []
                for c in range(3):
                    f = U[cur, c, x + 2, zu, :]
                    dx = combine(U[cur, c, x, zu, :], U[cur, c, x + 1, zu, :],
                                 U[cur, c, x + 3, zu, :], U[cur, c, x + 4, zu, :])
                    dr = combine(*[U[cur, c, x + 2, z0 + o:z0 + o + 8, :] for o in (6, 7, 9, 10)])
                    dy = combine(*shifted(f, pltpu.roll(halos[c], 126 - 4 * k, 1), lane))
                    g.append((dx + sx * dr, dy + sy * dr, st * dr))
                pressure = lam * (g[0][0] + g[1][1] + g[2][2])
                mu2 = mu + mu
                sxy = mu * (g[0][1] + g[1][0])
                syy = pressure + mu2 * g[1][1]
                syz = mu * (g[1][2] + g[2][1])
                S[0, x + 2, zu, :] = pressure + mu2 * g[0][0]
                S[1, x + 2, zu, :] = sxy
                S[2, x + 2, zu, :] = mu * (g[0][2] + g[2][0])
                S[3, x + 2, zu, :] = syy
                S[4, x + 2, zu, :] = syz
                S[5, x + 2, zu, :] = pressure + mu2 * g[2][2]
                here = (lane >> 2) == k
                for i, s in enumerate((sxy, syy, syz)):
                    packed[i] = jnp.where(here, pltpu.roll(s, 4 * k + 2, 1), packed[i])
            return tuple(packed)

        packed = lax.fori_loop(0, 8, stress, (zero8,) * 3)
        for i in range(3):
            PS[i] = packed[i]
        copies = exchange(s_planes, slice(0, 2), slice(10, 12), slice(2, 4), slice(8, 10), PS, HS, send_s, recv_s)
        for copy in copies:
            copy.wait()
        clear(s_planes)
        halos_s = [halo_of(HS, c) for c in range(3)]

        def forces(x, packed):
            packed = list(packed)
            for zb in range(4):
                z0 = zb * 8
                zs = slice(z0, z0 + 8)
                zu = slice(z0 + 8, z0 + 16)
                k = x * 4 + zb
                sx, sy, st, b = (MET[i, x, zs, :] for i in (0, 1, 2, 5))

                def d_x(i):
                    return combine(S[i, x, zu, :], S[i, x + 1, zu, :], S[i, x + 3, zu, :], S[i, x + 4, zu, :])

                def d_y(i, h):
                    f = S[i, x + 2, zu, :]
                    return combine(*shifted(f, pltpu.roll(h, 126 - 4 * k, 1), lane))

                dr = [combine(*[S[i, x + 2, z0 + o:z0 + o + 8, :] for o in (6, 7, 9, 10)]) for i in range(6)]
                acc = (
                    d_x(0) + sx * dr[0] + d_y(1, halos_s[0]) + sy * dr[1] + st * dr[2],
                    d_x(1) + sx * dr[1] + d_y(3, halos_s[1]) + sy * dr[3] + st * dr[4],
                    d_x(2) + sx * dr[2] + d_y(4, halos_s[2]) + sy * dr[4] + st * dr[5],
                )
                here = (lane >> 2) == k
                for c in range(3):
                    u = U[cur, c, x + 2, zu, :]
                    p = U[old, c, x + 2, zu, :]
                    fol = (u + u - p) + b * acc[c]
                    U[old, c, x + 2, zu, :] = fol
                    RATE[c, x, zs, :] = fol - p
                    packed[c] = jnp.where(here, pltpu.roll(fol, 4 * k + 2, 1), packed[c])
            return tuple(packed)

        packed = lax.fori_loop(0, 8, forces, (zero8,) * 3)
        for c in range(3):
            PU[c] = packed[c]
        return carry

    def sketch(n):
        lhs = jnp.concatenate(
            [RATE[c, 2 * xh, pl.ds(0, 16, stride=2), :] for xh in range(4) for c in range(3)], axis=0)
        SK[...] += jnp.dot(lhs, PE[n], precision=HIGH, preferred_element_type=F32)

    lax.fori_loop(0, STEPS, step, 0)
    sketch(STEPS - 1)
    for g in range(8):
        for xh in range(4):
            pieces[g, 6 * xh:6 * xh + 6, :] = SK[xh * 48 + 6 * g:xh * 48 + 6 * g + 6, :]

    final = STEPS % 2

    @pl.loop(0, 8)
    def _(x):
        for zb in range(4):
            for c in range(3):
                out[c, pl.ds(zb * 64 + x, 8, stride=8), :] = U[final, c, x + 2, zb * 8 + 8:zb * 8 + 16, :]


def wave(disp, vel, slopes, stretch, moduli, buoy, probes):
    return pl.pallas_call(
        wave_kernel,
        name="wave",
        out_shape=(jax.ShapeDtypeStruct((3, 256, 128), F32), jax.ShapeDtypeStruct((8, 24, 128), F32)),
        in_specs=[pl.BlockSpec(memory_space=VMEM)] * 7,
        out_specs=[pl.BlockSpec(memory_space=VMEM)] * 2,
        scratch_shapes=[
            pltpu.VMEM((2, 3, 12, ZP, 128), F32),
            pltpu.VMEM((6, 12, ZP, 128), F32),
            pltpu.VMEM((6, 8, 32, 128), F32),
            pltpu.VMEM((3, 8, 32, 128), F32),
            pltpu.VMEM((STEPS, 128, 128), F32),
            pltpu.VMEM((192, 128), F32),
            pltpu.VMEM((3, 8, 128), F32),
            pltpu.VMEM((3, 8, 128), F32),
            pltpu.VMEM((2, 3, 8, 128), F32),
            pltpu.VMEM((2, 3, 8, 128), F32),
            pltpu.SemaphoreType.DMA((4,)),
            pltpu.SemaphoreType.DMA((4,)),
            pltpu.SemaphoreType.DMA((4,)),
            pltpu.SemaphoreType.DMA((4,)),
        ],
        compiler_params=pltpu.CompilerParams(
            collective_id=0, has_side_effects=True, vmem_limit_bytes=32 * 1024 * 1024),
    )(disp, vel, slopes, stretch, moduli, buoy, probes)


def gram_kernel(pieces, tall, gram, RB, GL, RA, PA, RBB, GS,
                s0, r0, s1, r1, s2, r2, s3, r3):
    gx, gy = lax.axis_index("gx"), lax.axis_index("gy")
    core = lax.rem(gx, 2)
    pair = gx - core
    a_me = gy * 2 + core
    b_me = gx // 2

    def a_dev(a):
        return (pair + lax.rem(a, 2), a // 2)

    def b_dev(b):
        return (b * 2 + core, gy)

    barrier = pltpu.get_barrier_semaphore()

    @pl.loop(1, 16)
    def _(d):
        pl.semaphore_signal(barrier, inc=1, device_id=a_dev(lax.rem(a_me + d, 16)), device_id_type=MESH)
        pl.semaphore_signal(barrier, inc=1, device_id=b_dev(lax.rem(b_me + d, 16)), device_id_type=MESH)

    pl.semaphore_wait(barrier, 30)

    def copy0(g):
        return pltpu.make_async_remote_copy(
            src_ref=pieces.at[g], dst_ref=RB.at[gy], send_sem=s0.at[g], recv_sem=r0.at[gy],
            device_id=(gx, g), device_id_type=MESH)

    def wait0(g):
        return pltpu.make_async_remote_copy(
            src_ref=pieces.at[g], dst_ref=RB.at[g], send_sem=s0.at[g], recv_sem=r0.at[g],
            device_id=(gx, g), device_id_type=MESH)

    @pl.loop(1, 8)
    def _(d):
        copy0(lax.rem(gy + d, 8)).start()

    RB[gy] = pieces[gy]

    @pl.loop(1, 8)
    def _(d):
        wait0(lax.rem(gy + d, 8)).wait()

    total = RB[0]
    for g in range(1, 8):
        total = total + RB[g]
    tall[...] = total
    GL[...] = lax.dot_general(
        total, total, (((0,), (0,)), ((), ())), precision=HIGH, preferred_element_type=F32).reshape(16, 8, 128)

    def group(d, dev, me, src, dst, send, recv):
        def make(slot, peer):
            return pltpu.make_async_remote_copy(
                src_ref=src(peer), dst_ref=dst.at[slot], send_sem=send.at[peer], recv_sem=recv.at[slot],
                device_id=dev(peer), device_id_type=MESH)

        @pl.loop(1, 16)
        def _(d):
            make(me, lax.rem(me + d, 16)).start()

        def finish():
            @pl.loop(1, 16)
            def _(d):
                peer = lax.rem(me + d, 16)
                make(peer, peer).wait()

        return finish

    def summed(ref):
        parts = [ref[i] for i in range(16)]
        while len(parts) > 1:
            parts = [parts[i] + parts[i + 1] for i in range(0, len(parts), 2)]
        return parts[0]

    finish = group(0, a_dev, a_me, lambda p: GL.at[p], RA, s1, r1)
    RA[a_me] = GL[a_me]
    finish()
    part = summed(RA)
    PA[...] = part
    finish = group(0, b_dev, b_me, lambda p: PA, RBB, s2, r2)
    RBB[b_me] = part
    finish()
    whole = summed(RBB)
    GS[...] = whole
    finish = group(0, a_dev, a_me, lambda p: GS, gram, s3, r3)
    gram[a_me] = whole
    finish()


def gram_reduce(pieces):
    sem = pltpu.SemaphoreType.DMA
    return pl.pallas_call(
        gram_kernel,
        name="gram",
        out_shape=(jax.ShapeDtypeStruct((24, 128), F32), jax.ShapeDtypeStruct((16, 8, 128), F32)),
        in_specs=[pl.BlockSpec(memory_space=VMEM)],
        out_specs=[pl.BlockSpec(memory_space=VMEM)] * 2,
        scratch_shapes=[
            pltpu.VMEM((8, 24, 128), F32),
            pltpu.VMEM((16, 8, 128), F32),
            pltpu.VMEM((16, 8, 128), F32),
            pltpu.VMEM((8, 128), F32),
            pltpu.VMEM((16, 8, 128), F32),
            pltpu.VMEM((8, 128), F32),
            sem((8,)), sem((8,)), sem((16,)), sem((16,)), sem((16,)), sem((16,)), sem((16,)), sem((16,)),
        ],
        compiler_params=pltpu.CompilerParams(collective_id=1, has_side_effects=True),
    )(pieces)


def factor_kernel(scale, gram, tall, disp, basis, factor, out, sem):
    copy = pltpu.make_async_copy(disp, out, sem)
    copy.start()
    lane = lanes()
    sub = lax.broadcasted_iota(jnp.int32, (8, 128), 0)
    a = [gram[i] for i in range(16)]
    for j in range(128):
        b, s = divmod(j, 8)
        col = jnp.broadcast_to(a[b][:, j:j + 1], (8, 128))
        row = jnp.broadcast_to(a[b][s:s + 1, :], (8, 128))
        pivot = jnp.broadcast_to(col[s:s + 1, :], (8, 128))
        inv = 1.0 / pivot
        here = lane == j
        scaled = jnp.where(here, 1.0, row) * inv
        for i in range(b, 16):
            if i == b:
                if s == 7:
                    continue
                m = jnp.where(sub > s, col, 0.0)
                a[i] = jnp.where(here & (sub > s), 0.0, a[i]) - m * scaled
            else:
                m = jnp.broadcast_to(a[i][:, j:j + 1], (8, 128))
                a[i] = jnp.where(here, 0.0, a[i]) - m * scaled
    inverse = []
    for i in range(16):
        rows = sub + 8 * i
        diag = jnp.sum(jnp.where(lane == rows, a[i], 0.0), axis=1, keepdims=True)
        root = lax.rsqrt(diag)
        factor[8 * i:8 * i + 8, :] = jnp.where(lane >= rows, a[i], 0.0) * root
        inverse.append(jnp.where(lane == rows, 1.0, jnp.where(lane < rows, a[i], 0.0)) * (root * scale))
    inverse = jnp.concatenate(inverse, axis=0)
    q = lax.dot_general(
        tall[...], inverse, (((1,), (1,)), ((), ())), precision=HIGH, preferred_element_type=F32)
    for xh in range(4):
        basis[xh] = q[6 * xh:6 * xh + 6, :]
    copy.wait()


def finish(gram, tall, disp, scale):
    return pl.pallas_call(
        functools.partial(factor_kernel, scale),
        name="factor",
        out_shape=(
            jax.ShapeDtypeStruct((4, 6, 128), F32),
            jax.ShapeDtypeStruct((128, 128), F32),
            jax.ShapeDtypeStruct((3, 256, 128), F32),
        ),
        in_specs=[pl.BlockSpec(memory_space=VMEM)] * 2 + [pl.BlockSpec(memory_space=pl.ANY)],
        out_specs=[pl.BlockSpec(memory_space=VMEM)] * 2 + [pl.BlockSpec(memory_space=pl.ANY)],
        scratch_shapes=[pltpu.SemaphoreType.DMA],
    )(gram, tall, disp)


def shards(displacement, velocity, slopes, stretch, moduli, buoyancy, probes):
    moved, pieces = wave(
        displacement.reshape(3, 256, 128), velocity.reshape(3, 256, 128), slopes.reshape(2, 256, 128),
        stretch.reshape(256, 128), moduli.reshape(2, 256, 128), buoyancy.reshape(256, 128), probes)
    tall, gram = gram_reduce(pieces)
    rows = tall.shape[0] * lax.axis_size("gx") * lax.axis_size("gy")
    basis, factor, moved = finish(gram, tall, moved, math.sqrt(rows))
    return moved.reshape(3, 32, 8, 128), basis, factor


def solution(mesh):
    in_specs = (
        P(None, None, "gx", "gy"),
        P(None, None, "gx", "gy"),
        P(None, None, "gx", "gy"),
        P(None, "gx", "gy"),
        P(None, None, "gx", "gy"),
        P(None, "gx", "gy"),
        P(None, "gy", None),
    )
    out_specs = (P(None, None, "gx", "gy"), P("gx", "gy", None), P())
    return jax.shard_map(shards, mesh=mesh, in_specs=in_specs, out_specs=out_specs, check_vma=False)
```

time: 1210 us -> 124 us (0.10); the launches traced: 1190 us -> 124 us
  matrix products: 475 us -> 0 us
  waiting for transfers between devices: 362 us -> 0 us
  Pallas kernels: 0 us -> 114 us
  loops' own time: 98.3 us -> 0 us
  starting transfers between devices: 89 us -> 0 us
  local copies, waits for them, and re-layouts: 85.4 us -> 9.29 us
  other arithmetic: 68.3 us -> 0 us
  between operations: 15.9 us -> 0.68 us
    dot_general x646 -> x0, matrix products: 475 us -> none  [the longest x128 124 us: column_step(): column = jnp.dot(gram, picker, precision=lax.Precision.HIGHEST)]
    psum x1 -> x0, waiting for transfers between devices: 245 us -> none  [shards(): gram_whole = lax.psum(gram_local, ('gx', 'gy'))]
    pallas_call x0 -> x3, Pallas kernels: none -> 114 us  [the longest x1 64.6 us: wave(): pl.pallas_call(wave_kernel, name='wave', out_shape=(jax.ShapeDtypeStruct(...]
    another operation x2 -> x0, loops' own time: 98.3 us -> none  [the longest x1 94 us: lower_factor(): return lax.fori_loop(0, order, column_step, jnp.zeros_like(gram))]
    ppermute x32 -> x0, starting transfers between devices: 88.9 us -> none  [the longest x16 62.5 us: extended(): lax.ppermute(lax.slice_in_dim(block, block.shape[dim] - width, None, axis...]
    unnamed x3 -> x0, waiting for transfers between devices: 78.1 us -> none
    slice x30 -> x0, local copies, waits for them, and re-layouts: 41.1 us -> none  [the longest x12 18.5 us: extended(): lax.slice_in_dim(block, 0, width, axis=dim)]
    add x264 -> x0, other arithmetic: 39.3 us -> none  [the longest x128 13.4 us: row_step(): return inverse + picker[:, None] * fresh[None, :]]
  transfers between devices with their start and end apart: 34 -> 0, of which waited for: 17 -> 0; matrix products, arithmetic and copies ran while one was open for 5% -> 0% of each run, Pallas kernels for 0% -> 0%
where the time goes in v1:
time: 124 us
  Pallas kernels  114 us (92%)
  local copies, waits for them, and re-layouts  9.29 us (7%)
    pallas_call x1, Pallas kernels, wave(): pl.pallas_call(wave_kernel, name='wave', out_shape=(jax.ShapeDtypeStruct(...  64.6 us
    pallas_call x1, Pallas kernels, gram_reduce(): pl.pallas_call(gram_kernel, name='gram', out_shape=(jax.ShapeDtypeStruct(...  30.8 us
    pallas_call x1, Pallas kernels, finish(): pl.pallas_call(functools.partial(factor_kernel, scale), name='factor', ou...  18.7 us
    unnamed x19, local copies, waits for them, and re-layouts  9.29 us

profile of v1, /device:TPU:1, one launch (start us, length us, event | category | flops | bytes accessed | tf_op | source)
XLA Modules:
  0.0 124.1 jit_solution(7313633412892689623)
XLA Ops:
  0.6 0.0 copy-start.1
  0.6 1.0 copy-done.1
  1.6 0.0 copy-start.2
  1.6 1.0 copy-done.2
  2.6 0.0 copy-start.3
  2.6 0.9 copy-done.3
  3.6 0.0 copy-start.4
  3.6 0.9 copy-done.4
  4.5 0.0 copy-start.5
  4.5 0.9 copy-done.5
  5.4 0.0 copy-start.6
  5.4 0.9 copy-done.6
  6.3 0.0 copy-start.7
  6.3 0.9 copy-done.7
  7.2 64.6 %wave.1 = (f32[3,256,128]{2,1,0:T(8,128)S(1)}, f32[8,24,128]{2,1,0:T(8,128)S(1)}) custom-call(f32[3,256,128]{2,1,0:T(8,128)S(1)} %bitcast.7, f32[3,256,128]{2,1,0:T(8,128)S(1)} %bitcast.8, f32[2,256,128]{2,1,0:T(8,128)S(1)} %bitcast.9, f32[256,128]{1,0:T(8,128)S(1)} %bitcast.11, f32[2,256,128]{2,1,0:T(8,128)S(1)} %bitcast.10, f32[256,128]{1,0:T(8,128)S(1)} %bitcast.12, ...), custom_call_target="tpu_custom_call" | custom-call | tf_op jit(solution)/shard_map/wave/pallas_call | solution.py:254
  71.8 0.0 copy-start
  71.8 0.7 copy-done
  72.5 0.0 copy-start.8
  72.5 0.6 copy-done.8
  73.2 30.8 %gram.1 = (f32[24,128]{1,0:T(8,128)}, f32[16,8,128]{2,1,0:T(8,128)}) custom-call(f32[8,24,128]{2,1,0:T(8,128)} %copy-done.8), custom_call_target="tpu_custom_call" | custom-call | tf_op jit(solution)/shard_map/gram/pallas_call | solution.py:372
  104.0 18.7 %factor.1 = (f32[4,6,128]{2,1,0:T(8,128)}, f32[128,128]{1,0:T(8,128)}, f32[3,256,128]{2,1,0:T(8,128)}) custom-call(f32[16,8,128]{2,1,0:T(8,128)} %get-tuple-element.11.gram, f32[24,128]{1,0:T(8,128)} %get-tuple-element.12.tall, f32[3,256,128]{2,1,0:T(8,128)} %copy-done), custom_call_target="tpu_custom_call" | custom-call | tf_op jit(solution)/shard_map/factor/pallas_call | solution.py:430
  122.8 1.3 %copy.10 = f32[4,6,128]{2,0,1:T(4,128)} copy(f32[4,6,128]{2,1,0:T(8,128)} %get-tuple-element.18) | data formatting | bytes 24576
Async XLA Ops:
  0.6 1.0 copy-start.1
  1.6 1.0 copy-start.2
  2.6 0.9 copy-start.3
  3.6 0.9 copy-start.4
  4.5 0.9 copy-start.5
  5.4 0.9 copy-start.6
  6.3 0.9 copy-start.7
  71.8 0.7 copy-start
  72.5 0.6 copy-start.8

commit v2 on v1

v2 whole, which is shorter than its diff:
```python
import functools
import math

import jax
import jax.numpy as jnp
from jax import lax
from jax.experimental import pallas as pl
from jax.experimental.pallas import tpu as pltpu
from jax.sharding import PartitionSpec as P

STEPS = 4
DT = 0.12
MESH = pl.DeviceIdType.MESH
HIGH = lax.Precision.HIGHEST
F32 = jnp.float32
ZP = 48
VMEM = pltpu.MemorySpace.VMEM
VMEM_LIMIT = 63 * 1024 * 1024


def lanes():
    return lax.broadcasted_iota(jnp.int32, (8, 128), 1)


def shifted(f, h, lane):
    m2 = pltpu.roll(jnp.where(lane >= 126, h, f), 2, 1)
    m1 = pltpu.roll(jnp.where(lane >= 127, h, f), 1, 1)
    p1 = pltpu.roll(jnp.where(lane < 1, h, f), 127, 1)
    p2 = pltpu.roll(jnp.where(lane < 2, h, f), 126, 1)
    return m2, m1, p1, p2


def combine(m2, m1, p1, p2):
    return (m2 - p2) + 8.0 * (p1 - m1)


def wave_kernel(
    disp_hbm, vel_hbm, slopes_hbm, stretch_hbm, moduli_hbm, buoy_hbm, probes_hbm,
    tall, gram, out,
    disp, vel, slopes, stretch, moduli, buoy, probes,
    U, S, MET, RATE, PE, SK, PU, PS, HU, HS,
    PIECES, RB, GL, RA, PA, RBB, GS,
    load_sem, out_sem, send_x, recv_x, send_y, recv_y,
    s0, r0, s1, r1, s2, r2, s3, r3,
):
    gx, gy = lax.axis_index("gx"), lax.axis_index("gy")
    nx, ny = lax.axis_size("gx"), lax.axis_size("gy")
    left = (lax.rem(gx + nx - 1, nx), gy)
    right = (lax.rem(gx + 1, nx), gy)
    down = (gx, lax.rem(gy + ny - 1, ny))
    up = (gx, lax.rem(gy + 1, ny))
    has_left, has_right = gx > 0, gx < nx - 1
    core = lax.rem(gx, 2)
    pair = gx - core
    a_me = gy * 2 + core
    b_me = gx // 2

    def a_dev(a):
        return (pair + lax.rem(a, 2), a // 2)

    def b_dev(b):
        return (b * 2 + core, gy)

    loads = [
        pltpu.make_async_copy(src, dst, load_sem.at[i])
        for i, (src, dst) in enumerate((
            (disp_hbm, disp), (vel_hbm, vel), (slopes_hbm, slopes), (stretch_hbm, stretch),
            (moduli_hbm, moduli), (buoy_hbm, buoy), (probes_hbm, probes)))
    ]
    for copy in loads:
        copy.start()

    barrier = pltpu.get_barrier_semaphore()
    for peer in (left, right):
        pl.semaphore_signal(barrier, inc=1, device_id=peer, device_id_type=MESH)

    @pl.loop(1, 16)
    def _(d):
        pl.semaphore_signal(barrier, inc=1, device_id=a_dev(lax.rem(a_me + d, 16)), device_id_type=MESH)
        pl.semaphore_signal(barrier, inc=1, device_id=b_dev(lax.rem(b_me + d, 16)), device_id_type=MESH)

    lane = lanes()
    zero8 = jnp.zeros((8, 128), F32)
    low_part = (lane & 3) < 2

    @pl.loop(0, 12)
    def _(x):
        for s in range(2):
            for c in range(3):
                U[s, c, x, 0:8, :] = zero8
                U[s, c, x, 40:48, :] = zero8
        for c in range(6):
            S[c, x, 0:8, :] = zero8
            S[c, x, 40:48, :] = zero8

    def clear(x):
        for c in range(3):
            for z0 in range(8, 40, 8):
                U[0, c, x, z0:z0 + 8, :] = zero8
                U[1, c, x, z0:z0 + 8, :] = zero8
                S[c, x, z0:z0 + 8, :] = zero8

    @pl.when(gx == 0)
    def _():
        clear(0)
        clear(1)

    @pl.when(gx == nx - 1)
    def _():
        clear(10)
        clear(11)

    def x_copy(ref, kind, side):
        if side == 0:
            return pltpu.make_async_remote_copy(
                src_ref=ref(slice(2, 4)), dst_ref=ref(slice(10, 12)), send_sem=send_x.at[kind, 0],
                recv_sem=recv_x.at[kind, 0], device_id=left, device_id_type=MESH)
        return pltpu.make_async_remote_copy(
            src_ref=ref(slice(8, 10)), dst_ref=ref(slice(0, 2)), send_sem=send_x.at[kind, 1],
            recv_sem=recv_x.at[kind, 1], device_id=right, device_id_type=MESH)

    def x_start(ref, kind):
        @pl.when(has_left)
        def _():
            x_copy(ref, kind, 0).start()

        @pl.when(has_right)
        def _():
            x_copy(ref, kind, 1).start()

    def x_wait(ref, kind):
        @pl.when(has_right)
        def _():
            x_copy(ref, kind, 0).wait_recv()
            x_copy(ref, kind, 1).wait_send()

        @pl.when(has_left)
        def _():
            x_copy(ref, kind, 1).wait_recv()
            x_copy(ref, kind, 0).wait_send()

    def y_copies(packed, halo, kind, part):
        return [
            pltpu.make_async_remote_copy(
                src_ref=packed.at[part], dst_ref=halo.at[part, 1 - d], send_sem=send_y.at[kind, part, d],
                recv_sem=recv_y.at[kind, part, d], device_id=peer, device_id_type=MESH)
            for d, peer in enumerate((down, up))
        ]

    def y_send(values, packed, halo, kind, part):
        for c in range(3):
            packed[part, c] = values[c]
        for copy in y_copies(packed, halo, kind, part):
            copy.start()

    def y_wait(packed, halo, kind, part):
        for copy in y_copies(packed, halo, kind, part):
            copy.wait()
        result = []
        for c in range(3):
            lo = jnp.where(gy == 0, zero8, halo[part, 0, c])
            hi = jnp.where(gy == ny - 1, zero8, halo[part, 1, c])
            result.append(jnp.where(low_part, lo, hi))
        return result

    def u_planes(cur):
        return lambda xs: U.at[cur, :, xs, 8:40, :]

    def s_planes(xs):
        return S.at[0:3, xs, 8:40, :]

    INNER, EDGE = 0, 1

    def plane(part, i):
        return i + 2 if part == INNER else i + 4 * (i // 2)

    loads[0].wait()

    def load_u(part):
        def body(i, carry):
            x = plane(part, i)
            packed = list(carry)
            for zb in range(4):
                rows = pl.ds(zb * 64 + x, 8, stride=8)
                k = x * 4 + zb
                for c in range(3):
                    d = disp[c, rows, :]
                    U[0, c, x + 2, zb * 8 + 8:zb * 8 + 16, :] = d
                    packed[c] = jnp.where((lane >> 2) == k, pltpu.roll(d, 4 * k + 2, 1), packed[c])
            return tuple(packed)

        return lax.fori_loop(0, 4, body, (zero8,) * 3)

    first = [load_u(INNER), load_u(EDGE)]
    pl.semaphore_wait(barrier, 32)
    x_start(u_planes(0), 0)
    for part in (INNER, EDGE):
        y_send(first[part], PU, HU, 0, part)

    for copy in loads[1:]:
        copy.wait()

    @pl.loop(0, 8)
    def _(x):
        for zb in range(4):
            rows = pl.ds(zb * 64 + x, 8, stride=8)
            zs = slice(zb * 8, zb * 8 + 8)
            zu = slice(zb * 8 + 8, zb * 8 + 16)
            MET[0, x, zs, :] = slopes[0, rows, :]
            MET[1, x, zs, :] = slopes[1, rows, :]
            MET[2, x, zs, :] = stretch[rows, :]
            MET[3, x, zs, :] = moduli[0, rows, :] * (1.0 / 12.0)
            MET[4, x, zs, :] = moduli[1, rows, :] * (1.0 / 12.0)
            MET[5, x, zs, :] = buoy[rows, :] * (DT * DT / 12.0)
            for c in range(3):
                U[1, c, x + 2, zu, :] = U[0, c, x + 2, zu, :] - DT * vel[c, rows, :]

    for n in range(STEPS):
        PE[n] = jnp.zeros((128, 128), F32)
        PE[n, pl.ds(0, 64, stride=2), :] = probes[n] * (1.0 / (2.0 * DT))
    SK[...] = jnp.zeros_like(SK)

    def sketch(n, part):
        for xh in ((1, 2) if part == INNER else (0, 3)):
            lhs = jnp.concatenate([RATE[c, 2 * xh, pl.ds(0, 16, stride=2), :] for c in range(3)], axis=0)
            rows = slice(48 * xh, 48 * xh + 48)
            SK[rows, :] += jnp.dot(lhs, PE[n], precision=HIGH, preferred_element_type=F32)

    def stress(cur, part, halos):
        def body(i, packed):
            x = plane(part, i)
            packed = list(packed)
            for zb in range(4):
                z0 = zb * 8
                zs = slice(z0, z0 + 8)
                zu = slice(z0 + 8, z0 + 16)
                k = x * 4 + zb
                sx, sy, st = MET[0, x, zs, :], MET[1, x, zs, :], MET[2, x, zs, :]
                lam, mu = MET[3, x, zs, :], MET[4, x, zs, :]
                g = []
                for c in range(3):
                    f = U[cur, c, x + 2, zu, :]
                    dx = combine(U[cur, c, x, zu, :], U[cur, c, x + 1, zu, :],
                                 U[cur, c, x + 3, zu, :], U[cur, c, x + 4, zu, :])
                    dr = combine(*[U[cur, c, x + 2, z0 + o:z0 + o + 8, :] for o in (6, 7, 9, 10)])
                    dy = combine(*shifted(f, pltpu.roll(halos[c], 126 - 4 * k, 1), lane))
                    g.append((dx + sx * dr, dy + sy * dr, st * dr))
                pressure = lam * (g[0][0] + g[1][1] + g[2][2])
                mu2 = mu + mu
                sxy = mu * (g[0][1] + g[1][0])
                syy = pressure + mu2 * g[1][1]
                syz = mu * (g[1][2] + g[2][1])
                S[0, x + 2, zu, :] = pressure + mu2 * g[0][0]
                S[1, x + 2, zu, :] = sxy
                S[2, x + 2, zu, :] = mu * (g[0][2] + g[2][0])
                S[3, x + 2, zu, :] = syy
                S[4, x + 2, zu, :] = syz
                S[5, x + 2, zu, :] = pressure + mu2 * g[2][2]
                here = (lane >> 2) == k
                for i, s in enumerate((sxy, syy, syz)):
                    packed[i] = jnp.where(here, pltpu.roll(s, 4 * k + 2, 1), packed[i])
            return tuple(packed)

        return lax.fori_loop(0, 4, body, (zero8,) * 3)

    def forces(cur, part, halos):
        old = 1 - cur

        def body(i, packed):
            x = plane(part, i)
            packed = list(packed)
            for zb in range(4):
                z0 = zb * 8
                zs = slice(z0, z0 + 8)
                zu = slice(z0 + 8, z0 + 16)
                k = x * 4 + zb
                sx, sy, st, b = (MET[i, x, zs, :] for i in (0, 1, 2, 5))

                def d_x(i):
                    return combine(S[i, x, zu, :], S[i, x + 1, zu, :], S[i, x + 3, zu, :], S[i, x + 4, zu, :])

                def d_y(i, h):
                    f = S[i, x + 2, zu, :]
                    return combine(*shifted(f, pltpu.roll(h, 126 - 4 * k, 1), lane))

                dr = [combine(*[S[i, x + 2, z0 + o:z0 + o + 8, :] for o in (6, 7, 9, 10)]) for i in range(6)]
                acc = (
                    d_x(0) + sx * dr[0] + d_y(1, halos[0]) + sy * dr[1] + st * dr[2],
                    d_x(1) + sx * dr[1] + d_y(3, halos[1]) + sy * dr[3] + st * dr[4],
                    d_x(2) + sx * dr[2] + d_y(4, halos[2]) + sy * dr[4] + st * dr[5],
                )
                here = (lane >> 2) == k
                for c in range(3):
                    u = U[cur, c, x + 2, zu, :]
                    p = U[old, c, x + 2, zu, :]
                    fol = (u + u - p) + b * acc[c]
                    U[old, c, x + 2, zu, :] = fol
                    RATE[c, x, zs, :] = fol - p
                    packed[c] = jnp.where(here, pltpu.roll(fol, 4 * k + 2, 1), packed[c])
            return tuple(packed)

        return lax.fori_loop(0, 4, body, (zero8,) * 3)

    def step(n, carry):
        cur = lax.rem(n, 2)
        more = n < STEPS - 1
        packed = stress(cur, INNER, y_wait(PU, HU, 0, INNER))
        y_send(packed, PS, HS, 1, INNER)

        @pl.when(n > 0)
        def _():
            sketch(n - 1, EDGE)

        halos = y_wait(PU, HU, 0, EDGE)
        x_wait(u_planes(cur), 0)
        packed = stress(cur, EDGE, halos)
        x_start(s_planes, 1)
        y_send(packed, PS, HS, 1, EDGE)

        packed = forces(cur, INNER, y_wait(PS, HS, 1, INNER))

        @pl.when(more)
        def _():
            y_send(packed, PU, HU, 0, INNER)

        sketch(n, INNER)
        halos = y_wait(PS, HS, 1, EDGE)
        x_wait(s_planes, 1)
        packed_edge = forces(cur, EDGE, halos)

        @pl.when(more)
        def _():
            x_start(u_planes(1 - cur), 0)
            y_send(packed_edge, PU, HU, 0, EDGE)

        return carry

    lax.fori_loop(0, STEPS, step, 0)
    sketch(STEPS - 1, EDGE)
    for g in range(8):
        for xh in range(4):
            PIECES[g, 6 * xh:6 * xh + 6, :] = SK[xh * 48 + 6 * g:xh * 48 + 6 * g + 6, :]

    def piece(g, slot):
        return pltpu.make_async_remote_copy(
            src_ref=PIECES.at[g], dst_ref=RB.at[slot], send_sem=s0.at[g], recv_sem=r0.at[slot],
            device_id=(gx, g), device_id_type=MESH)

    @pl.loop(1, 8)
    def _(d):
        piece(lax.rem(gy + d, 8), gy).start()

    RB[gy] = PIECES[gy]

    final = STEPS % 2

    @pl.loop(0, 8)
    def _(x):
        for zb in range(4):
            for c in range(3):
                disp[c, pl.ds(zb * 64 + x, 8, stride=8), :] = U[final, c, x + 2, zb * 8 + 8:zb * 8 + 16, :]

    leave = pltpu.make_async_copy(disp, out, out_sem)
    leave.start()

    @pl.loop(1, 8)
    def _(d):
        g = lax.rem(gy + d, 8)
        piece(g, g).wait()

    total = RB[0]
    for g in range(1, 8):
        total = total + RB[g]
    tall[...] = total
    GL[...] = lax.dot_general(
        total, total, (((0,), (0,)), ((), ())), precision=HIGH, preferred_element_type=F32).reshape(16, 8, 128)

    def group(dev, me, src, dst, send, recv):
        def make(slot, peer):
            return pltpu.make_async_remote_copy(
                src_ref=src(peer), dst_ref=dst.at[slot], send_sem=send.at[peer], recv_sem=recv.at[slot],
                device_id=dev(peer), device_id_type=MESH)

        @pl.loop(1, 16)
        def _(d):
            make(me, lax.rem(me + d, 16)).start()

        def finish():
            @pl.loop(1, 16)
            def _(d):
                peer = lax.rem(me + d, 16)
                make(peer, peer).wait()

        return finish

    def summed(ref):
        parts = [ref[i] for i in range(16)]
        while len(parts) > 1:
            parts = [parts[i] + parts[i + 1] for i in range(0, len(parts), 2)]
        return parts[0]

    finish = group(a_dev, a_me, lambda p: GL.at[p], RA, s1, r1)
    RA[a_me] = GL[a_me]
    finish()
    part = summed(RA)
    PA[...] = part
    finish = group(b_dev, b_me, lambda p: PA, RBB, s2, r2)
    RBB[b_me] = part
    finish()
    whole = summed(RBB)
    GS[...] = whole
    finish = group(a_dev, a_me, lambda p: GS, gram, s3, r3)
    gram[a_me] = whole
    finish()
    leave.wait()


def wave(disp, vel, slopes, stretch, moduli, buoy, probes):
    sem = pltpu.SemaphoreType.DMA
    buffers = [
        (3, 256, 128), (3, 256, 128), (2, 256, 128), (256, 128), (2, 256, 128), (256, 128), (STEPS, 64, 128),
        (2, 3, 12, ZP, 128), (6, 12, ZP, 128), (6, 8, 32, 128), (3, 8, 32, 128), (STEPS, 128, 128), (192, 128),
        (2, 3, 8, 128), (2, 3, 8, 128), (2, 2, 3, 8, 128), (2, 2, 3, 8, 128),
        (8, 24, 128), (8, 24, 128), (16, 8, 128), (16, 8, 128), (8, 128), (16, 8, 128), (8, 128),
    ]
    sems = [(7,), (), (2, 2), (2, 2), (2, 2, 2), (2, 2, 2)] + [(8,)] * 2 + [(16,)] * 6
    return pl.pallas_call(
        wave_kernel,
        name="wave",
        out_shape=(
            jax.ShapeDtypeStruct((24, 128), F32),
            jax.ShapeDtypeStruct((16, 8, 128), F32),
            jax.ShapeDtypeStruct((3, 256, 128), F32),
        ),
        in_specs=[pl.BlockSpec(memory_space=pltpu.MemorySpace.HBM)] * 7,
        out_specs=[pl.BlockSpec(memory_space=VMEM)] * 2 + [pl.BlockSpec(memory_space=pltpu.MemorySpace.HBM)],
        scratch_shapes=[pltpu.VMEM(shape, F32) for shape in buffers] + [sem(shape) for shape in sems],
        compiler_params=pltpu.CompilerParams(
            collective_id=0, has_side_effects=True, vmem_limit_bytes=VMEM_LIMIT),
    )(disp, vel, slopes, stretch, moduli, buoy, probes)


def factor_kernel(scale, gram, tall, disp, basis, factor, out, sem):
    copy = pltpu.make_async_copy(disp, out, sem)
    copy.start()
    lane = lanes()
    sub = lax.broadcasted_iota(jnp.int32, (8, 128), 0)
    a = [gram[i] for i in range(16)]
    for j in range(128):
        b, s = divmod(j, 8)
        col = jnp.broadcast_to(a[b][:, j:j + 1], (8, 128))
        row = jnp.broadcast_to(a[b][s:s + 1, :], (8, 128))
        pivot = jnp.broadcast_to(col[s:s + 1, :], (8, 128))
        inv = 1.0 / pivot
        here = lane == j
        scaled = jnp.where(here, 1.0, row) * inv
        for i in range(b, 16):
            if i == b:
                if s == 7:
                    continue
                m = jnp.where(sub > s, col, 0.0)
                a[i] = jnp.where(here & (sub > s), 0.0, a[i]) - m * scaled
            else:
                m = jnp.broadcast_to(a[i][:, j:j + 1], (8, 128))
                a[i] = jnp.where(here, 0.0, a[i]) - m * scaled
    inverse = []
    for i in range(16):
        rows = sub + 8 * i
        diag = jnp.sum(jnp.where(lane == rows, a[i], 0.0), axis=1, keepdims=True)
        root = lax.rsqrt(diag)
        factor[8 * i:8 * i + 8, :] = jnp.where(lane >= rows, a[i], 0.0) * root
        inverse.append(jnp.where(lane == rows, 1.0, jnp.where(lane < rows, a[i], 0.0)) * (root * scale))
    inverse = jnp.concatenate(inverse, axis=0)
    q = lax.dot_general(
        tall[...], inverse, (((1,), (1,)), ((), ())), precision=HIGH, preferred_element_type=F32)
    for xh in range(4):
        for r in range(6):
            basis[r, xh:xh + 1, :] = q[6 * xh + r:6 * xh + r + 1, :]
    copy.wait()


def finish(gram, tall, disp, scale):
    return pl.pallas_call(
        functools.partial(factor_kernel, scale),
        name="factor",
        out_shape=(
            jax.ShapeDtypeStruct((6, 4, 128), F32),
            jax.ShapeDtypeStruct((128, 128), F32),
            jax.ShapeDtypeStruct((3, 256, 128), F32),
        ),
        in_specs=[pl.BlockSpec(memory_space=VMEM)] * 2 + [pl.BlockSpec(memory_space=pltpu.MemorySpace.HBM)],
        out_specs=[pl.BlockSpec(memory_space=VMEM)] * 2 + [pl.BlockSpec(memory_space=pltpu.MemorySpace.HBM)],
        scratch_shapes=[pltpu.SemaphoreType.DMA],
        compiler_params=pltpu.CompilerParams(vmem_limit_bytes=VMEM_LIMIT),
    )(gram, tall, disp)


def shards(displacement, velocity, slopes, stretch, moduli, buoyancy, probes):
    tall, gram, moved = wave(
        displacement.reshape(3, 256, 128), velocity.reshape(3, 256, 128), slopes.reshape(2, 256, 128),
        stretch.reshape(256, 128), moduli.reshape(2, 256, 128), buoyancy.reshape(256, 128), probes)
    rows = tall.shape[0] * lax.axis_size("gx") * lax.axis_size("gy")
    basis, factor, moved = finish(gram, tall, moved, math.sqrt(rows))
    return moved.reshape(3, 32, 8, 128), jnp.transpose(basis, (1, 0, 2)), factor


def solution(mesh):
    in_specs = (
        P(None, None, "gx", "gy"),
        P(None, None, "gx", "gy"),
        P(None, None, "gx", "gy"),
        P(None, "gx", "gy"),
        P(None, None, "gx", "gy"),
        P(None, "gx", "gy"),
        P(None, "gy", None),
    )
    out_specs = (P(None, None, "gx", "gy"), P("gx", "gy", None), P())
    return jax.shard_map(shards, mesh=mesh, in_specs=in_specs, out_specs=out_specs, check_vma=False)
```

time: 124 us -> 95.9 us (0.77)
  Pallas kernels: 114 us -> 95.2 us
  local copies, waits for them, and re-layouts: 9.29 us -> 0 us
    pallas_call x1 -> x0, Pallas kernels: 30.8 us -> none  [gram_reduce(): pl.pallas_call(gram_kernel, name='gram', out_shape=(jax.ShapeDtypeStruct(...]
    pallas_call x1, Pallas kernels: 64.6 us -> 76.4 us  [wave(): pl.pallas_call(wave_kernel, name='wave', out_shape=(jax.ShapeDtypeStruct(...]
    unnamed x19 -> x0, local copies, waits for them, and re-layouts: 9.29 us -> none
where the time goes in v2:
time: 95.9 us; the launch traced here: 95.8 us
  Pallas kernels  95.2 us (99%)
    pallas_call x1, Pallas kernels, wave(): pl.pallas_call(wave_kernel, name='wave', out_shape=(jax.ShapeDtypeStruct(...  76.4 us
    pallas_call x1, Pallas kernels, finish(): pl.pallas_call(functools.partial(factor_kernel, scale), name='factor', ou...  18.7 us

profile of v2, /device:TPU:1, one launch (start us, length us, event | category | flops | bytes accessed | tf_op | source)
XLA Modules:
  0.0 95.8 jit_solution(8773873665746035019)
XLA Ops:
  0.6 76.4 %wave.1 = (f32[24,128]{1,0:T(8,128)}, f32[16,8,128]{2,1,0:T(8,128)}, f32[3,256,128]{2,1,0:T(8,128)}) custom-call(f32[3,256,128]{2,1,0:T(8,128)} %bitcast.8, f32[3,256,128]{2,1,0:T(8,128)} %bitcast.9, f32[2,256,128]{2,1,0:T(8,128)} %bitcast.10, f32[256,128]{1,0:T(8,128)} %bitcast.12, f32[2,256,128]{2,1,0:T(8,128)} %bitcast.11, f32[256,128]{1,0:T(8,128)} %bitcast.13, ...), custom_call_target="tpu_custom_call" | custom-call | tf_op jit(solution)/shard_map/wave/pallas_call | solution.py:427
  77.0 18.7 %factor.1 = (f32[6,4,128]{2,1,0:T(4,128)}, f32[128,128]{1,0:T(8,128)}, f32[3,256,128]{2,1,0:T(8,128)}) custom-call(f32[16,8,128]{2,1,0:T(8,128)} %get-tuple-element.9.gram, f32[24,128]{1,0:T(8,128)} %get-tuple-element.10.tall, f32[3,256,128]{2,1,0:T(8,128)} %get-tuple-element.11.disp), custom_call_target="tpu_custom_call" | custom-call | tf_op jit(solution)/shard_map/factor/pallas_call | solution.py:483

commit v3 on v2

--- a/solution.py
+++ b/solution.py
@@ -13,6 +13,7 @@
 MESH = pl.DeviceIdType.MESH
 HIGH = lax.Precision.HIGHEST
 F32 = jnp.float32
+BF16 = jnp.bfloat16
 ZP = 48
 VMEM = pltpu.MemorySpace.VMEM
 VMEM_LIMIT = 63 * 1024 * 1024
@@ -34,11 +35,18 @@
     return (m2 - p2) + 8.0 * (p1 - m1)
 
 
+def split(x):
+    hi = x.astype(BF16)
+    rest = x - hi.astype(F32)
+    mid = rest.astype(BF16)
+    return hi, mid, (rest - mid.astype(F32)).astype(BF16)
+
+
 def wave_kernel(
     disp_hbm, vel_hbm, slopes_hbm, stretch_hbm, moduli_hbm, buoy_hbm, probes_hbm,
     tall, gram, out,
     disp, vel, slopes, stretch, moduli, buoy, probes,
-    U, S, MET, RATE, PE, SK, PU, PS, HU, HS,
+    PE, spread, U, S, MET, RATE, SK, PU, PS, HU, HS,
     PIECES, RB, GL, RA, PA, RBB, GS,
     load_sem, out_sem, send_x, recv_x, send_y, recv_y,
     s0, r0, s1, r1, s2, r2, s3, r3,
@@ -215,91 +223,103 @@
             for c in range(3):
                 U[1, c, x + 2, zu, :] = U[0, c, x + 2, zu, :] - DT * vel[c, rows, :]
 
+    spread[...] = jnp.zeros((128, 128), F32)
     for n in range(STEPS):
-        PE[n] = jnp.zeros((128, 128), F32)
-        PE[n, pl.ds(0, 64, stride=2), :] = probes[n] * (1.0 / (2.0 * DT))
+        spread[pl.ds(0, 64, stride=2), :] = probes[n] * (1.0 / (2.0 * DT))
+        hi, mid, lo = split(spread[...])
+        for i, term in enumerate((hi, mid, hi, lo, mid, hi)):
+            PE[n, 128 * i:128 * i + 128, :] = term
     SK[...] = jnp.zeros_like(SK)
 
     def sketch(n, part):
-        for xh in ((1, 2) if part == INNER else (0, 3)):
-            lhs = jnp.concatenate([RATE[c, 2 * xh, pl.ds(0, 16, stride=2), :] for c in range(3)], axis=0)
-            rows = slice(48 * xh, 48 * xh + 48)
-            SK[rows, :] += jnp.dot(lhs, PE[n], precision=HIGH, preferred_element_type=F32)
+        where = (1, 2) if part == INNER else (0, 3)
+        hi, mid, lo = split(jnp.concatenate(
+            [RATE[c, 2 * xh, pl.ds(0, 16, stride=2), :] for xh in where for c in range(3)], axis=0))
+        term = jnp.dot(
+            jnp.concatenate([hi, hi, mid, hi, mid, lo], axis=1), PE[n], preferred_element_type=F32)
+        for i, xh in enumerate(where):
+            SK[48 * xh:48 * xh + 48, :] += term[48 * i:48 * i + 48, :]
+
+    def over_planes(part, planes, cell, put):
+        def body(i, packed):
+            cells = [(plane(part, i * planes + j), zb) for j in range(planes) for zb in range(4)]
+            values = [cell(x, zb) for x, zb in cells]
+            packed = list(packed)
+            for (x, zb), value in zip(cells, values):
+                edge = put(x, zb, value)
+                k = x * 4 + zb
+                here = (lane >> 2) == k
+                for c in range(3):
+                    packed[c] = jnp.where(here, pltpu.roll(edge[c], 4 * k + 2, 1), packed[c])
+            return tuple(packed)
+
+        if planes == 4:
+            return body(0, (zero8,) * 3)
+        return lax.fori_loop(0, 4 // planes, body, (zero8,) * 3)
 
     def stress(cur, part, halos):
-        def body(i, packed):
-            x = plane(part, i)
-            packed = list(packed)
-            for zb in range(4):
-                z0 = zb * 8
-                zs = slice(z0, z0 + 8)
-                zu = slice(z0 + 8, z0 + 16)
-                k = x * 4 + zb
-                sx, sy, st = MET[0, x, zs, :], MET[1, x, zs, :], MET[2, x, zs, :]
-                lam, mu = MET[3, x, zs, :], MET[4, x, zs, :]
-                g = []
-                for c in range(3):
-                    f = U[cur, c, x + 2, zu, :]
-                    dx = combine(U[cur, c, x, zu, :], U[cur, c, x + 1, zu, :],
-                                 U[cur, c, x + 3, zu, :], U[cur, c, x + 4, zu, :])
-                    dr = combine(*[U[cur, c, x + 2, z0 + o:z0 + o + 8, :] for o in (6, 7, 9, 10)])
-                    dy = combine(*shifted(f, pltpu.roll(halos[c], 126 - 4 * k, 1), lane))
-                    g.append((dx + sx * dr, dy + sy * dr, st * dr))
-                pressure = lam * (g[0][0] + g[1][1] + g[2][2])
-                mu2 = mu + mu
-                sxy = mu * (g[0][1] + g[1][0])
-                syy = pressure + mu2 * g[1][1]
-                syz = mu * (g[1][2] + g[2][1])
-                S[0, x + 2, zu, :] = pressure + mu2 * g[0][0]
-                S[1, x + 2, zu, :] = sxy
-                S[2, x + 2, zu, :] = mu * (g[0][2] + g[2][0])
-                S[3, x + 2, zu, :] = syy
-                S[4, x + 2, zu, :] = syz
-                S[5, x + 2, zu, :] = pressure + mu2 * g[2][2]
-                here = (lane >> 2) == k
-                for i, s in enumerate((sxy, syy, syz)):
-                    packed[i] = jnp.where(here, pltpu.roll(s, 4 * k + 2, 1), packed[i])
-            return tuple(packed)
-
-        return lax.fori_loop(0, 4, body, (zero8,) * 3)
+        def cell(x, zb):
+            z0 = zb * 8
+            zs, zu = slice(z0, z0 + 8), slice(z0 + 8, z0 + 16)
+            k = x * 4 + zb
+            sx, sy, st = MET[0, x, zs, :], MET[1, x, zs, :], MET[2, x, zs, :]
+            lam, mu = MET[3, x, zs, :], MET[4, x, zs, :]
+            g = []
+            for c in range(3):
+                f = U[cur, c, x + 2, zu, :]
+                dx = combine(U[cur, c, x, zu, :], U[cur, c, x + 1, zu, :],
+                             U[cur, c, x + 3, zu, :], U[cur, c, x + 4, zu, :])
+                dr = combine(*[U[cur, c, x + 2, z0 + o:z0 + o + 8, :] for o in (6, 7, 9, 10)])
+                dy = combine(*shifted(f, pltpu.roll(halos[c], 126 - 4 * k, 1), lane))
+                g.append((dx + sx * dr, dy + sy * dr, st * dr))
+            pressure = lam * (g[0][0] + g[1][1] + g[2][2])
+            mu2 = mu + mu
+            return (pressure + mu2 * g[0][0], mu * (g[0][1] + g[1][0]), mu * (g[0][2] + g[2][0]),
+                    pressure + mu2 * g[1][1], mu * (g[1][2] + g[2][1]), pressure + mu2 * g[2][2])
+
+        def put(x, zb, value):
+            for j in range(6):
+                S[j, x + 2, zb * 8 + 8:zb * 8 + 16, :] = value[j]
+            return value[1], value[3], value[4]
+
+        return over_planes(part, 2, cell, put)
 
     def forces(cur, part, halos):
         old = 1 - cur
 
-        def body(i, packed):
-            x = plane(part, i)
-            packed = list(packed)
-            for zb in range(4):
-                z0 = zb * 8
-                zs = slice(z0, z0 + 8)
-                zu = slice(z0 + 8, z0 + 16)
-                k = x * 4 + zb
-                sx, sy, st, b = (MET[i, x, zs, :] for i in (0, 1, 2, 5))
-
-                def d_x(i):
-                    return combine(S[i, x, zu, :], S[i, x + 1, zu, :], S[i, x + 3, zu, :], S[i, x + 4, zu, :])
-
-                def d_y(i, h):
-                    f = S[i, x + 2, zu, :]
-                    return combine(*shifted(f, pltpu.roll(h, 126 - 4 * k, 1), lane))
-
-                dr = [combine(*[S[i, x + 2, z0 + o:z0 + o + 8, :] for o in (6, 7, 9, 10)]) for i in range(6)]
-                acc = (
-                    d_x(0) + sx * dr[0] + d_y(1, halos[0]) + sy * dr[1] + st * dr[2],
-                    d_x(1) + sx * dr[1] + d_y(3, halos[1]) + sy * dr[3] + st * dr[4],
-                    d_x(2) + sx * dr[2] + d_y(4, halos[2]) + sy * dr[4] + st * dr[5],
-                )
-                here = (lane >> 2) == k
-                for c in range(3):
-                    u = U[cur, c, x + 2, zu, :]
-                    p = U[old, c, x + 2, zu, :]
-                    fol = (u + u - p) + b * acc[c]
-                    U[old, c, x + 2, zu, :] = fol
-                    RATE[c, x, zs, :] = fol - p
-                    packed[c] = jnp.where(here, pltpu.roll(fol, 4 * k + 2, 1), packed[c])
-            return tuple(packed)
-
-        return lax.fori_loop(0, 4, body, (zero8,) * 3)
+        def cell(x, zb):
+            z0 = zb * 8
+            zs, zu = slice(z0, z0 + 8), slice(z0 + 8, z0 + 16)
+            k = x * 4 + zb
+            sx, sy, st, b = (MET[j, x, zs, :] for j in (0, 1, 2, 5))
+
+            def d_x(j):
+                return combine(S[j, x, zu, :], S[j, x + 1, zu, :], S[j, x + 3, zu, :], S[j, x + 4, zu, :])
+
+            def d_y(j, h):
+                return combine(*shifted(S[j, x + 2, zu, :], pltpu.roll(h, 126 - 4 * k, 1), lane))
+
+            dr = [combine(*[S[j, x + 2, z0 + o:z0 + o + 8, :] for o in (6, 7, 9, 10)]) for j in range(6)]
+            acc = (
+                d_x(0) + sx * dr[0] + d_y(1, halos[0]) + sy * dr[1] + st * dr[2],
+                d_x(1) + sx * dr[1] + d_y(3, halos[1]) + sy * dr[3] + st * dr[4],
+                d_x(2) + sx * dr[2] + d_y(4, halos[2]) + sy * dr[4] + st * dr[5],
+            )
+            moved = []
+            for c in range(3):
+                u, p = U[cur, c, x + 2, zu, :], U[old, c, x + 2, zu, :]
+                fol = (u + u - p) + b * acc[c]
+                moved.append((fol, fol - p))
+            return moved
+
+        def put(x, zb, value):
+            z0 = zb * 8
+            for c in range(3):
+                U[old, c, x + 2, z0 + 8:z0 + 16, :] = value[c][0]
+                RATE[c, x, z0:z0 + 8, :] = value[c][1]
+            return [v[0] for v in value]
+
+        return over_planes(part, 2, cell, put)
 
     def step(n, carry):
         cur = lax.rem(n, 2)
@@ -419,7 +439,7 @@
     sem = pltpu.SemaphoreType.DMA
     buffers = [
         (3, 256, 128), (3, 256, 128), (2, 256, 128), (256, 128), (2, 256, 128), (256, 128), (STEPS, 64, 128),
-        (2, 3, 12, ZP, 128), (6, 12, ZP, 128), (6, 8, 32, 128), (3, 8, 32, 128), (STEPS, 128, 128), (192, 128),
+        (128, 128), (2, 3, 12, ZP, 128), (6, 12, ZP, 128), (6, 8, 32, 128), (3, 8, 32, 128), (192, 128),
         (2, 3, 8, 128), (2, 3, 8, 128), (2, 2, 3, 8, 128), (2, 2, 3, 8, 128),
         (8, 24, 128), (8, 24, 128), (16, 8, 128), (16, 8, 128), (8, 128), (16, 8, 128), (8, 128),
     ]
@@ -434,35 +454,57 @@
         ),
         in_specs=[pl.BlockSpec(memory_space=pltpu.MemorySpace.HBM)] * 7,
         out_specs=[pl.BlockSpec(memory_space=VMEM)] * 2 + [pl.BlockSpec(memory_space=pltpu.MemorySpace.HBM)],
-        scratch_shapes=[pltpu.VMEM(shape, F32) for shape in buffers] + [sem(shape) for shape in sems],
+        scratch_shapes=[pltpu.VMEM(shape, F32) for shape in buffers[:7]]
+        + [pltpu.VMEM((STEPS, 768, 128), BF16)]
+        + [pltpu.VMEM(shape, F32) for shape in buffers[7:]] + [sem(shape) for shape in sems],
         compiler_params=pltpu.CompilerParams(
             collective_id=0, has_side_effects=True, vmem_limit_bytes=VMEM_LIMIT),
     )(disp, vel, slopes, stretch, moduli, buoy, probes)
 
 
-def factor_kernel(scale, gram, tall, disp, basis, factor, out, sem):
-    copy = pltpu.make_async_copy(disp, out, sem)
-    copy.start()
+def factor_kernel(scale, gram, tall, disp, basis, factor, out, stage, sem):
+    enter = pltpu.make_async_copy(disp, stage, sem.at[0])
+    leave = pltpu.make_async_copy(stage, out, sem.at[1])
+    enter.start()
     lane = lanes()
     sub = lax.broadcasted_iota(jnp.int32, (8, 128), 0)
     a = [gram[i] for i in range(16)]
-    for j in range(128):
-        b, s = divmod(j, 8)
-        col = jnp.broadcast_to(a[b][:, j:j + 1], (8, 128))
-        row = jnp.broadcast_to(a[b][s:s + 1, :], (8, 128))
-        pivot = jnp.broadcast_to(col[s:s + 1, :], (8, 128))
-        inv = 1.0 / pivot
-        here = lane == j
-        scaled = jnp.where(here, 1.0, row) * inv
-        for i in range(b, 16):
-            if i == b:
-                if s == 7:
-                    continue
-                m = jnp.where(sub > s, col, 0.0)
-                a[i] = jnp.where(here & (sub > s), 0.0, a[i]) - m * scaled
-            else:
-                m = jnp.broadcast_to(a[i][:, j:j + 1], (8, 128))
-                a[i] = jnp.where(here, 0.0, a[i]) - m * scaled
+    for b in range(16):
+        if b == 4:
+            enter.wait()
+            leave.start()
+        j0 = 8 * b
+        inside = (lane >= j0) & (lane < j0 + 8)
+        cols = [jnp.broadcast_to(a[b][:, j0 + t:j0 + t + 1], (8, 128)) for t in range(8)]
+        d = [[jnp.broadcast_to(cols[t][s:s + 1, :], (8, 128)) if t >= s else None for t in range(8)]
+             for s in range(8)]
+        inv = [None] * 8
+        m = [[None] * 8 for _ in range(8)]
+        for s in range(8):
+            inv[s] = 1.0 / d[s][s]
+            for t in range(s + 1, 8):
+                m[s][t] = d[s][t] * inv[s]
+                for q in range(t, 8):
+                    d[t][q] = d[t][q] - m[s][t] * d[s][q]
+        unit = [None] * 8
+        fresh = a[b]
+        for t in range(8):
+            x = jnp.broadcast_to(a[b][t:t + 1, :], (8, 128))
+            for s in range(t):
+                x = jnp.where(lane == j0 + s, 0.0, x) - m[s][t] * unit[s]
+            unit[t] = jnp.where(lane == j0 + t, 1.0, x)
+            fresh = jnp.where(sub == t, x, fresh)
+        a[b] = fresh
+        below = [jnp.where((lane > j0 + t) & inside, 0.0, unit[t]) for t in range(8)]
+        for i in range(b + 1, 16):
+            c = [jnp.broadcast_to(a[i][:, j0 + s:j0 + s + 1], (8, 128)) for s in range(8)]
+            x = jnp.where(inside, 0.0, a[i])
+            for s in range(8):
+                ms = c[s] * inv[s]
+                for t in range(s + 1, 8):
+                    c[t] = c[t] - ms * d[s][t]
+                x = x - ms * below[s]
+            a[i] = x
     inverse = []
     for i in range(16):
         rows = sub + 8 * i
@@ -476,7 +518,7 @@
     for xh in range(4):
         for r in range(6):
             basis[r, xh:xh + 1, :] = q[6 * xh + r:6 * xh + r + 1, :]
-    copy.wait()
+    leave.wait()
 
 
 def finish(gram, tall, disp, scale):
@@ -490,7 +532,7 @@
         ),
         in_specs=[pl.BlockSpec(memory_space=VMEM)] * 2 + [pl.BlockSpec(memory_space=pltpu.MemorySpace.HBM)],
         out_specs=[pl.BlockSpec(memory_space=VMEM)] * 2 + [pl.BlockSpec(memory_space=pltpu.MemorySpace.HBM)],
-        scratch_shapes=[pltpu.SemaphoreType.DMA],
+        scratch_shapes=[pltpu.VMEM((3, 256, 128), F32), pltpu.SemaphoreType.DMA((2,))],
         compiler_params=pltpu.CompilerParams(vmem_limit_bytes=VMEM_LIMIT),
     )(gram, tall, disp)
 

time: 95.9 us -> 79 us (0.82)
  Pallas kernels: 95.2 us -> 78.2 us
    pallas_call x1, Pallas kernels: 18.7 us -> 6.79 us  [finish(): pl.pallas_call(functools.partial(factor_kernel, scale), name='factor', ou...]
    pallas_call x1, Pallas kernels: 76.4 us -> 71.4 us  [wave(): pl.pallas_call(wave_kernel, name='wave', out_shape=(jax.ShapeDtypeStruct(...]
where the time goes in v3:
time: 79 us; the launch traced here: 78.8 us
  Pallas kernels  78.2 us (99%)
    pallas_call x1, Pallas kernels, wave(): pl.pallas_call(wave_kernel, name='wave', out_shape=(jax.ShapeDtypeStruct(...  71.4 us
    pallas_call x1, Pallas kernels, finish(): pl.pallas_call(functools.partial(factor_kernel, scale), name='factor', ou...  6.79 us

profile of v3, /device:TPU:1, one launch (start us, length us, event | category | flops | bytes accessed | tf_op | source)
XLA Modules:
  0.0 78.8 jit_solution(12191035830625357729)
XLA Ops:
  0.6 71.4 %wave.1 = (f32[24,128]{1,0:T(8,128)}, f32[16,8,128]{2,1,0:T(8,128)}, f32[3,256,128]{2,1,0:T(8,128)}) custom-call(f32[3,256,128]{2,1,0:T(8,128)} %bitcast.8, f32[3,256,128]{2,1,0:T(8,128)} %bitcast.9, f32[2,256,128]{2,1,0:T(8,128)} %bitcast.10, f32[256,128]{1,0:T(8,128)} %bitcast.12, f32[2,256,128]{2,1,0:T(8,128)} %bitcast.11, f32[256,128]{1,0:T(8,128)} %bitcast.13, ...), custom_call_target="tpu_custom_call" | custom-call | tf_op jit(solution)/shard_map/wave/pallas_call | solution.py:447
  72.1 6.8 %factor.1 = (f32[6,4,128]{2,1,0:T(4,128)}, f32[128,128]{1,0:T(8,128)}, f32[3,256,128]{2,1,0:T(8,128)}) custom-call(f32[16,8,128]{2,1,0:T(8,128)} %get-tuple-element.9.gram, f32[24,128]{1,0:T(8,128)} %get-tuple-element.10.tall, f32[3,256,128]{2,1,0:T(8,128)} %get-tuple-element.11.disp), custom_call_target="tpu_custom_call" | custom-call | tf_op jit(solution)/shard_map/factor/pallas_call | solution.py:525

commit v4 on v3

--- a/solution.py
+++ b/solution.py
@@ -57,8 +57,8 @@
     right = (lax.rem(gx + 1, nx), gy)
     down = (gx, lax.rem(gy + ny - 1, ny))
     up = (gx, lax.rem(gy + 1, ny))
-    has_left, has_right = gx > 0, gx < nx - 1
     core = lax.rem(gx, 2)
+    has_off = (gx > 0) & (gx < nx - 1)
     pair = gx - core
     a_me = gy * 2 + core
     b_me = gx // 2
@@ -118,34 +118,32 @@
         clear(10)
         clear(11)
 
-    def x_copy(ref, kind, side):
-        if side == 0:
-            return pltpu.make_async_remote_copy(
-                src_ref=ref(slice(2, 4)), dst_ref=ref(slice(10, 12)), send_sem=send_x.at[kind, 0],
-                recv_sem=recv_x.at[kind, 0], device_id=left, device_id_type=MESH)
+    INNER, ON, OFF = 0, 1, 2
+
+    def side(part):
+        return core if part == OFF else 1 - core
+
+    def x_copy(ref, kind, part):
+        s = side(part)
         return pltpu.make_async_remote_copy(
-            src_ref=ref(slice(8, 10)), dst_ref=ref(slice(0, 2)), send_sem=send_x.at[kind, 1],
-            recv_sem=recv_x.at[kind, 1], device_id=right, device_id_type=MESH)
-
-    def x_start(ref, kind):
-        @pl.when(has_left)
-        def _():
-            x_copy(ref, kind, 0).start()
-
-        @pl.when(has_right)
-        def _():
-            x_copy(ref, kind, 1).start()
-
-    def x_wait(ref, kind):
-        @pl.when(has_right)
-        def _():
-            x_copy(ref, kind, 0).wait_recv()
-            x_copy(ref, kind, 1).wait_send()
-
-        @pl.when(has_left)
-        def _():
-            x_copy(ref, kind, 1).wait_recv()
-            x_copy(ref, kind, 0).wait_send()
+            src_ref=ref(pl.ds(2 + 6 * s, 2)), dst_ref=ref(pl.ds(10 - 10 * s, 2)), send_sem=send_x.at[kind, part - 1],
+            recv_sem=recv_x.at[kind, part - 1], device_id=(gx - 1 + 2 * s, gy), device_id_type=MESH)
+
+    def x_start(ref, kind, part):
+        if part == ON:
+            x_copy(ref, kind, part).start()
+        else:
+            @pl.when(has_off)
+            def _():
+                x_copy(ref, kind, part).start()
+
+    def x_wait(ref, kind, part):
+        if part == ON:
+            x_copy(ref, kind, part).wait()
+        else:
+            @pl.when(has_off)
+            def _():
+                x_copy(ref, kind, part).wait()
 
     def y_copies(packed, halo, kind, part):
         return [
@@ -177,10 +175,8 @@
     def s_planes(xs):
         return S.at[0:3, xs, 8:40, :]
 
-    INNER, EDGE = 0, 1
-
     def plane(part, i):
-        return i + 2 if part == INNER else i + 4 * (i // 2)
+        return i + 2 if part == INNER else i + 6 * side(part)
 
     loads[0].wait()
 
@@ -197,12 +193,13 @@
                     packed[c] = jnp.where((lane >> 2) == k, pltpu.roll(d, 4 * k + 2, 1), packed[c])
             return tuple(packed)
 
-        return lax.fori_loop(0, 4, body, (zero8,) * 3)
-
-    first = [load_u(INNER), load_u(EDGE)]
+        return lax.fori_loop(0, 4 if part == INNER else 2, body, (zero8,) * 3)
+
+    first = [load_u(INNER), load_u(ON), load_u(OFF)]
     pl.semaphore_wait(barrier, 32)
-    x_start(u_planes(0), 0)
-    for part in (INNER, EDGE):
+    for part in (OFF, ON):
+        x_start(u_planes(0), 0, part)
+    for part in (INNER, OFF, ON):
         y_send(first[part], PU, HU, 0, part)
 
     for copy in loads[1:]:
@@ -231,8 +228,8 @@
             PE[n, 128 * i:128 * i + 128, :] = term
     SK[...] = jnp.zeros_like(SK)
 
-    def sketch(n, part):
-        where = (1, 2) if part == INNER else (0, 3)
+    def sketch(n, outer):
+        where = (0, 3) if outer else (1, 2)
         hi, mid, lo = split(jnp.concatenate(
             [RATE[c, 2 * xh, pl.ds(0, 16, stride=2), :] for xh in where for c in range(3)], axis=0))
         term = jnp.dot(
@@ -253,7 +250,7 @@
                     packed[c] = jnp.where(here, pltpu.roll(edge[c], 4 * k + 2, 1), packed[c])
             return tuple(packed)
 
-        if planes == 4:
+        if part != INNER:
             return body(0, (zero8,) * 3)
         return lax.fori_loop(0, 4 // planes, body, (zero8,) * 3)
 
@@ -329,13 +326,14 @@
 
         @pl.when(n > 0)
         def _():
-            sketch(n - 1, EDGE)
-
-        halos = y_wait(PU, HU, 0, EDGE)
-        x_wait(u_planes(cur), 0)
-        packed = stress(cur, EDGE, halos)
-        x_start(s_planes, 1)
-        y_send(packed, PS, HS, 1, EDGE)
+            sketch(n - 1, True)
+
+        for part in (ON, OFF):
+            halos = y_wait(PU, HU, 0, part)
+            x_wait(u_planes(cur), 0, part)
+            packed = stress(cur, part, halos)
+            x_start(s_planes, 1, part)
+            y_send(packed, PS, HS, 1, part)
 
         packed = forces(cur, INNER, y_wait(PS, HS, 1, INNER))
 
@@ -343,32 +341,37 @@
         def _():
             y_send(packed, PU, HU, 0, INNER)
 
-        sketch(n, INNER)
-        halos = y_wait(PS, HS, 1, EDGE)
-        x_wait(s_planes, 1)
-        packed_edge = forces(cur, EDGE, halos)
-
-        @pl.when(more)
-        def _():
-            x_start(u_planes(1 - cur), 0)
-            y_send(packed_edge, PU, HU, 0, EDGE)
+        sketch(n, False)
+        for part in (ON, OFF):
+            halos = y_wait(PS, HS, 1, part)
+            x_wait(s_planes, 1, part)
+            packed = forces(cur, part, halos)
+
+            @pl.when(more)
+            def _():
+                x_start(u_planes(1 - cur), 0, part)
+                y_send(packed, PU, HU, 0, part)
 
         return carry
 
     lax.fori_loop(0, STEPS, step, 0)
-    sketch(STEPS - 1, EDGE)
+    sketch(STEPS - 1, True)
     for g in range(8):
         for xh in range(4):
             PIECES[g, 6 * xh:6 * xh + 6, :] = SK[xh * 48 + 6 * g:xh * 48 + 6 * g + 6, :]
+
+    def far_first(i, half):
+        step = (i + 1) // 2
+        return half + step * (2 * lax.rem(i, 2) - 1)
 
     def piece(g, slot):
         return pltpu.make_async_remote_copy(
             src_ref=PIECES.at[g], dst_ref=RB.at[slot], send_sem=s0.at[g], recv_sem=r0.at[slot],
             device_id=(gx, g), device_id_type=MESH)
 
-    @pl.loop(1, 8)
-    def _(d):
-        piece(lax.rem(gy + d, 8), gy).start()
+    @pl.loop(0, 7)
+    def _(i):
+        piece(lax.rem(gy + far_first(i, 4), 8), gy).start()
 
     RB[gy] = PIECES[gy]
 
@@ -392,8 +395,11 @@
     for g in range(1, 8):
         total = total + RB[g]
     tall[...] = total
+    hi, mid, lo = (term.astype(F32) for term in split(total))
     GL[...] = lax.dot_general(
-        total, total, (((0,), (0,)), ((), ())), precision=HIGH, preferred_element_type=F32).reshape(16, 8, 128)
+        jnp.concatenate([hi, hi, mid, hi, mid, lo], axis=0).astype(BF16),
+        jnp.concatenate([hi, mid, hi, lo, mid, hi], axis=0).astype(BF16),
+        (((0,), (0,)), ((), ())), preferred_element_type=F32).reshape(16, 8, 128)
 
     def group(dev, me, src, dst, send, recv):
         def make(slot, peer):
@@ -401,9 +407,9 @@
                 src_ref=src(peer), dst_ref=dst.at[slot], send_sem=send.at[peer], recv_sem=recv.at[slot],
                 device_id=dev(peer), device_id_type=MESH)
 
-        @pl.loop(1, 16)
-        def _(d):
-            make(me, lax.rem(me + d, 16)).start()
+        @pl.loop(0, 15)
+        def _(i):
+            make(me, lax.rem(me + far_first(i, 8), 16)).start()
 
         def finish():
             @pl.loop(1, 16)
@@ -419,18 +425,18 @@
             parts = [parts[i] + parts[i + 1] for i in range(0, len(parts), 2)]
         return parts[0]
 
-    finish = group(a_dev, a_me, lambda p: GL.at[p], RA, s1, r1)
-    RA[a_me] = GL[a_me]
+    finish = group(b_dev, b_me, lambda p: GL.at[p], RA, s1, r1)
+    RA[b_me] = GL[b_me]
     finish()
     part = summed(RA)
     PA[...] = part
-    finish = group(b_dev, b_me, lambda p: PA, RBB, s2, r2)
-    RBB[b_me] = part
+    finish = group(a_dev, a_me, lambda p: PA, RBB, s2, r2)
+    RBB[a_me] = part
     finish()
     whole = summed(RBB)
     GS[...] = whole
-    finish = group(a_dev, a_me, lambda p: GS, gram, s3, r3)
-    gram[a_me] = whole
+    finish = group(b_dev, b_me, lambda p: GS, gram, s3, r3)
+    gram[b_me] = whole
     finish()
     leave.wait()
 
@@ -440,10 +446,10 @@
     buffers = [
         (3, 256, 128), (3, 256, 128), (2, 256, 128), (256, 128), (2, 256, 128), (256, 128), (STEPS, 64, 128),
         (128, 128), (2, 3, 12, ZP, 128), (6, 12, ZP, 128), (6, 8, 32, 128), (3, 8, 32, 128), (192, 128),
-        (2, 3, 8, 128), (2, 3, 8, 128), (2, 2, 3, 8, 128), (2, 2, 3, 8, 128),
+        (3, 3, 8, 128), (3, 3, 8, 128), (3, 2, 3, 8, 128), (3, 2, 3, 8, 128),
         (8, 24, 128), (8, 24, 128), (16, 8, 128), (16, 8, 128), (8, 128), (16, 8, 128), (8, 128),
     ]
-    sems = [(7,), (), (2, 2), (2, 2), (2, 2, 2), (2, 2, 2)] + [(8,)] * 2 + [(16,)] * 6
+    sems = [(7,), (), (2, 2), (2, 2), (2, 3, 2), (2, 3, 2)] + [(8,)] * 2 + [(16,)] * 6
     return pl.pallas_call(
         wave_kernel,
         name="wave",

time: 79 us -> 75.1 us (0.951)
  Pallas kernels: 78.2 us -> 74.3 us
    pallas_call x1, Pallas kernels: 71.4 us -> 67.5 us  [wave(): pl.pallas_call(wave_kernel, name='wave', out_shape=(jax.ShapeDtypeStruct(...]
where the time goes in v4:
time: 75.1 us; the launch traced here: 75 us
  Pallas kernels  74.3 us (99%)
    pallas_call x1, Pallas kernels, wave(): pl.pallas_call(wave_kernel, name='wave', out_shape=(jax.ShapeDtypeStruct(...  67.5 us
    pallas_call x1, Pallas kernels, finish(): pl.pallas_call(functools.partial(factor_kernel, scale), name='factor', ou...  6.79 us

profile of v4, /device:TPU:1, one launch (start us, length us, event | category | flops | bytes accessed | tf_op | source)
XLA Modules:
  0.0 75.0 jit_solution(2042958412323812721)
XLA Ops:
  0.6 67.5 %wave.1 = (f32[24,128]{1,0:T(8,128)}, f32[16,8,128]{2,1,0:T(8,128)}, f32[3,256,128]{2,1,0:T(8,128)}) custom-call(f32[3,256,128]{2,1,0:T(8,128)} %bitcast.8, f32[3,256,128]{2,1,0:T(8,128)} %bitcast.9, f32[2,256,128]{2,1,0:T(8,128)} %bitcast.10, f32[256,128]{1,0:T(8,128)} %bitcast.12, f32[2,256,128]{2,1,0:T(8,128)} %bitcast.11, f32[256,128]{1,0:T(8,128)} %bitcast.13, ...), custom_call_target="tpu_custom_call" | custom-call | tf_op jit(solution)/shard_map/wave/pallas_call | solution.py:453
  68.2 6.8 %factor.1 = (f32[6,4,128]{2,1,0:T(4,128)}, f32[128,128]{1,0:T(8,128)}, f32[3,256,128]{2,1,0:T(8,128)}) custom-call(f32[16,8,128]{2,1,0:T(8,128)} %get-tuple-element.9.gram, f32[24,128]{1,0:T(8,128)} %get-tuple-element.10.tall, f32[3,256,128]{2,1,0:T(8,128)} %get-tuple-element.11.disp), custom_call_target="tpu_custom_call" | custom-call | tf_op jit(solution)/shard_map/factor/pallas_call | solution.py:531

commit v5 on v4

--- a/solution.py
+++ b/solution.py
@@ -16,7 +16,7 @@
 BF16 = jnp.bfloat16
 ZP = 48
 VMEM = pltpu.MemorySpace.VMEM
-VMEM_LIMIT = 63 * 1024 * 1024
+VMEM_LIMIT = 24 * 1024 * 1024
 
 
 def lanes():
@@ -48,7 +48,7 @@
     disp, vel, slopes, stretch, moduli, buoy, probes,
     PE, spread, U, S, MET, RATE, SK, PU, PS, HU, HS,
     PIECES, RB, GL, RA, PA, RBB, GS,
-    load_sem, out_sem, send_x, recv_x, send_y, recv_y,
+    load_sem, send_x, recv_x, send_y, recv_y,
     s0, r0, s1, r1, s2, r2, s3, r3,
 ):
     gx, gy = lax.axis_index("gx"), lax.axis_index("gy")
@@ -69,6 +69,10 @@
     def b_dev(b):
         return (b * 2 + core, gy)
 
+    def far_first(i, half):
+        step = (i + 1) // 2
+        return half + step * (2 * lax.rem(i, 2) - 1)
+
     loads = [
         pltpu.make_async_copy(src, dst, load_sem.at[i])
         for i, (src, dst) in enumerate((
@@ -79,13 +83,15 @@
         copy.start()
 
     barrier = pltpu.get_barrier_semaphore()
+
+    @pl.loop(0, 15)
+    def _(i):
+        d = far_first(i, 8)
+        pl.semaphore_signal(barrier, inc=1, device_id=a_dev(lax.rem(a_me + d, 16)), device_id_type=MESH)
+        pl.semaphore_signal(barrier, inc=1, device_id=b_dev(lax.rem(b_me + d, 16)), device_id_type=MESH)
+
     for peer in (left, right):
         pl.semaphore_signal(barrier, inc=1, device_id=peer, device_id_type=MESH)
-
-    @pl.loop(1, 16)
-    def _(d):
-        pl.semaphore_signal(barrier, inc=1, device_id=a_dev(lax.rem(a_me + d, 16)), device_id_type=MESH)
-        pl.semaphore_signal(barrier, inc=1, device_id=b_dev(lax.rem(b_me + d, 16)), device_id_type=MESH)
 
     lane = lanes()
     zero8 = jnp.zeros((8, 128), F32)
@@ -360,10 +366,6 @@
         for xh in range(4):
             PIECES[g, 6 * xh:6 * xh + 6, :] = SK[xh * 48 + 6 * g:xh * 48 + 6 * g + 6, :]
 
-    def far_first(i, half):
-        step = (i + 1) // 2
-        return half + step * (2 * lax.rem(i, 2) - 1)
-
     def piece(g, slot):
         return pltpu.make_async_remote_copy(
             src_ref=PIECES.at[g], dst_ref=RB.at[slot], send_sem=s0.at[g], recv_sem=r0.at[slot],
@@ -381,10 +383,7 @@
     def _(x):
         for zb in range(4):
             for c in range(3):
-                disp[c, pl.ds(zb * 64 + x, 8, stride=8), :] = U[final, c, x + 2, zb * 8 + 8:zb * 8 + 16, :]
-
-    leave = pltpu.make_async_copy(disp, out, out_sem)
-    leave.start()
+                out[c, pl.ds(zb * 64 + x, 8, stride=8), :] = U[final, c, x + 2, zb * 8 + 8:zb * 8 + 16, :]
 
     @pl.loop(1, 8)
     def _(d):
@@ -438,7 +437,6 @@
     finish = group(b_dev, b_me, lambda p: GS, gram, s3, r3)
     gram[b_me] = whole
     finish()
-    leave.wait()
 
 
 def wave(disp, vel, slopes, stretch, moduli, buoy, probes):
@@ -449,7 +447,7 @@
         (3, 3, 8, 128), (3, 3, 8, 128), (3, 2, 3, 8, 128), (3, 2, 3, 8, 128),
         (8, 24, 128), (8, 24, 128), (16, 8, 128), (16, 8, 128), (8, 128), (16, 8, 128), (8, 128),
     ]
-    sems = [(7,), (), (2, 2), (2, 2), (2, 3, 2), (2, 3, 2)] + [(8,)] * 2 + [(16,)] * 6
+    sems = [(7,), (2, 2), (2, 2), (2, 3, 2), (2, 3, 2)] + [(8,)] * 2 + [(16,)] * 6
     return pl.pallas_call(
         wave_kernel,
         name="wave",
@@ -459,26 +457,23 @@
             jax.ShapeDtypeStruct((3, 256, 128), F32),
         ),
         in_specs=[pl.BlockSpec(memory_space=pltpu.MemorySpace.HBM)] * 7,
-        out_specs=[pl.BlockSpec(memory_space=VMEM)] * 2 + [pl.BlockSpec(memory_space=pltpu.MemorySpace.HBM)],
+        out_specs=[pl.BlockSpec(memory_space=VMEM)] * 3,
         scratch_shapes=[pltpu.VMEM(shape, F32) for shape in buffers[:7]]
         + [pltpu.VMEM((STEPS, 768, 128), BF16)]
         + [pltpu.VMEM(shape, F32) for shape in buffers[7:]] + [sem(shape) for shape in sems],
         compiler_params=pltpu.CompilerParams(
             collective_id=0, has_side_effects=True, vmem_limit_bytes=VMEM_LIMIT),
-    )(disp, vel, slopes, stretch, moduli, buoy, probes)
-
-
-def factor_kernel(scale, gram, tall, disp, basis, factor, out, stage, sem):
-    enter = pltpu.make_async_copy(disp, stage, sem.at[0])
-    leave = pltpu.make_async_copy(stage, out, sem.at[1])
-    enter.start()
+    )(*[pltpu.with_memory_space_constraint(x, pltpu.MemorySpace.HBM)
+        for x in (disp, vel, slopes, stretch, moduli, buoy, probes)])
+
+
+def factor_kernel(scale, gram, tall, disp, basis, factor, out, sem):
+    leave = pltpu.make_async_copy(disp, out, sem)
+    leave.start()
     lane = lanes()
     sub = lax.broadcasted_iota(jnp.int32, (8, 128), 0)
     a = [gram[i] for i in range(16)]
     for b in range(16):
-        if b == 4:
-            enter.wait()
-            leave.start()
         j0 = 8 * b
         inside = (lane >= j0) & (lane < j0 + 8)
         cols = [jnp.broadcast_to(a[b][:, j0 + t:j0 + t + 1], (8, 128)) for t in range(8)]
@@ -536,9 +531,9 @@
             jax.ShapeDtypeStruct((128, 128), F32),
             jax.ShapeDtypeStruct((3, 256, 128), F32),
         ),
-        in_specs=[pl.BlockSpec(memory_space=VMEM)] * 2 + [pl.BlockSpec(memory_space=pltpu.MemorySpace.HBM)],
+        in_specs=[pl.BlockSpec(memory_space=VMEM)] * 3,
         out_specs=[pl.BlockSpec(memory_space=VMEM)] * 2 + [pl.BlockSpec(memory_space=pltpu.MemorySpace.HBM)],
-        scratch_shapes=[pltpu.VMEM((3, 256, 128), F32), pltpu.SemaphoreType.DMA((2,))],
+        scratch_shapes=[pltpu.SemaphoreType.DMA],
         compiler_params=pltpu.CompilerParams(vmem_limit_bytes=VMEM_LIMIT),
     )(gram, tall, disp)
 

time: 75.1 us -> 73 us (0.972)
  Pallas kernels: 74.3 us -> 72.3 us
    pallas_call x1, Pallas kernels: 6.79 us -> 5.42 us  [finish(): pl.pallas_call(functools.partial(factor_kernel, scale), name='factor', ou...]
where the time goes in v5:
time: 73 us; the launch traced here: 72.9 us
  Pallas kernels  72.3 us (99%)
    pallas_call x1, Pallas kernels, wave(): pl.pallas_call(wave_kernel, name='wave', out_shape=(jax.ShapeDtypeStruct(...  66.9 us
    pallas_call x1, Pallas kernels, finish(): pl.pallas_call(functools.partial(factor_kernel, scale), name='factor', ou...  5.42 us

profile of v5, /device:TPU:1, one launch (start us, length us, event | category | flops | bytes accessed | tf_op | source)
XLA Modules:
  0.0 72.9 jit_solution(10779550202044209041)
XLA Ops:
  0.6 66.9 %wave.1 = (f32[24,128]{1,0:T(8,128)S(1)}, f32[16,8,128]{2,1,0:T(8,128)S(1)}, f32[3,256,128]{2,1,0:T(8,128)S(1)}) custom-call(f32[3,256,128]{2,1,0:T(8,128)} %bitcast.8, f32[3,256,128]{2,1,0:T(8,128)} %bitcast.9, f32[2,256,128]{2,1,0:T(8,128)} %bitcast.10, f32[256,128]{1,0:T(8,128)} %bitcast.12, f32[2,256,128]{2,1,0:T(8,128)} %bitcast.11, ...), custom_call_target="tpu_custom_call" | custom-call | tf_op jit(solution)/shard_map/wave/pallas_call | solution.py:451
  67.5 5.4 %factor.1 = (f32[6,4,128]{2,1,0:T(4,128)}, f32[128,128]{1,0:T(8,128)}, f32[3,256,128]{2,1,0:T(8,128)}) custom-call(f32[16,8,128]{2,1,0:T(8,128)S(1)} %get-tuple-element.9.gram, f32[24,128]{1,0:T(8,128)S(1)} %get-tuple-element.10.tall, f32[3,256,128]{2,1,0:T(8,128)S(1)} %get-tuple-element.11.disp), custom_call_target="tpu_custom_call" | custom-call | tf_op jit(solution)/shard_map/factor/pallas_call | solution.py:526

commit v6 on v5

--- a/solution.py
+++ b/solution.py
@@ -47,8 +47,8 @@
     tall, gram, out,
     disp, vel, slopes, stretch, moduli, buoy, probes,
     PE, spread, U, S, MET, RATE, SK, PU, PS, HU, HS,
-    PIECES, RB, GL, RA, PA, RBB, GS,
-    load_sem, send_x, recv_x, send_y, recv_y,
+    SA, AH, MH, PIECES, RB, GL, RA, PA, RBB, GS,
+    load_sem, send_u, recv_u, send_s, recv_s, send_y, recv_y, send_a, recv_a, moduli_sem,
     s0, r0, s1, r1, s2, r2, s3, r3,
 ):
     gx, gy = lax.axis_index("gx"), lax.axis_index("gy")
@@ -107,6 +107,16 @@
             S[c, x, 0:8, :] = zero8
             S[c, x, 40:48, :] = zero8
 
+    @pl.when(jnp.logical_not(has_off))
+    def _():
+        for i in range(2):
+            for z0 in range(0, 32, 8):
+                for c in range(3):
+                    AH[0, c, i, z0:z0 + 8, :] = zero8
+                    AH[1, c, i, z0:z0 + 8, :] = zero8
+                for c in range(2):
+                    MH[c, i, z0:z0 + 8, :] = zero8
+
     def clear(x):
         for c in range(3):
             for z0 in range(8, 40, 8):
@@ -129,27 +139,46 @@
     def side(part):
         return core if part == OFF else 1 - core
 
-    def x_copy(ref, kind, part):
+    def u_copy(cur, part):
         s = side(part)
+        index = 2 * cur + part - 1
         return pltpu.make_async_remote_copy(
-            src_ref=ref(pl.ds(2 + 6 * s, 2)), dst_ref=ref(pl.ds(10 - 10 * s, 2)), send_sem=send_x.at[kind, part - 1],
-            recv_sem=recv_x.at[kind, part - 1], device_id=(gx - 1 + 2 * s, gy), device_id_type=MESH)
-
-    def x_start(ref, kind, part):
+            src_ref=U.at[cur, :, pl.ds(2 + 6 * s, 2), 8:40, :], dst_ref=U.at[cur, :, pl.ds(10 - 10 * s, 2), 8:40, :],
+            send_sem=send_u.at[index], recv_sem=recv_u.at[index],
+            device_id=(gx - 1 + 2 * s, gy), device_id_type=MESH)
+
+    def s_copy():
+        s = side(ON)
+        return pltpu.make_async_remote_copy(
+            src_ref=S.at[0:3, pl.ds(2 + 6 * s, 2), 8:40, :], dst_ref=S.at[0:3, pl.ds(10 - 10 * s, 2), 8:40, :],
+            send_sem=send_s, recv_sem=recv_s, device_id=(gx - 1 + 2 * s, gy), device_id_type=MESH)
+
+    def far_copy(src, dst, send, recv):
+        return pltpu.make_async_remote_copy(
+            src_ref=src, dst_ref=dst, send_sem=send, recv_sem=recv,
+            device_id=(gx - 1 + 2 * turn, gy), device_id_type=MESH)
+
+    def partial_copy(parity):
+        return far_copy(SA, AH.at[parity], send_a.at[parity], recv_a.at[parity])
+
+    def moduli_copy():
+        return far_copy(MET.at[3:5, pl.ds(6 * turn, 2)], MH, moduli_sem.at[0], moduli_sem.at[1])
+
+    def u_start(cur, part):
         if part == ON:
-            x_copy(ref, kind, part).start()
+            u_copy(cur, part).start()
         else:
             @pl.when(has_off)
             def _():
-                x_copy(ref, kind, part).start()
-
-    def x_wait(ref, kind, part):
+                u_copy(cur, part).start()
+
+    def u_wait(cur, part):
         if part == ON:
-            x_copy(ref, kind, part).wait()
+            u_copy(cur, part).wait()
         else:
             @pl.when(has_off)
             def _():
-                x_copy(ref, kind, part).wait()
+                u_copy(cur, part).wait()
 
     def y_copies(packed, halo, kind, part):
         return [
@@ -175,13 +204,13 @@
             result.append(jnp.where(low_part, lo, hi))
         return result
 
-    def u_planes(cur):
-        return lambda xs: U.at[cur, :, xs, 8:40, :]
-
-    def s_planes(xs):
-        return S.at[0:3, xs, 8:40, :]
+    turn = core
+    outermost, second, inward = 7 * turn, 1 + 5 * turn, 1 - 2 * turn
+    sign = jnp.where(turn == 0, 1.0, -1.0).astype(F32)
 
     def plane(part, i):
+        if part == OFF:
+            return second if i == 1 else outermost
         return i + 2 if part == INNER else i + 6 * side(part)
 
     loads[0].wait()
@@ -199,12 +228,14 @@
                     packed[c] = jnp.where((lane >> 2) == k, pltpu.roll(d, 4 * k + 2, 1), packed[c])
             return tuple(packed)
 
+        if part == OFF:
+            return body(1, body(0, (zero8,) * 3))
         return lax.fori_loop(0, 4 if part == INNER else 2, body, (zero8,) * 3)
 
     first = [load_u(INNER), load_u(ON), load_u(OFF)]
     pl.semaphore_wait(barrier, 32)
     for part in (OFF, ON):
-        x_start(u_planes(0), 0, part)
+        u_start(0, part)
     for part in (INNER, OFF, ON):
         y_send(first[part], PU, HU, 0, part)
 
@@ -226,6 +257,10 @@
             for c in range(3):
                 U[1, c, x + 2, zu, :] = U[0, c, x + 2, zu, :] - DT * vel[c, rows, :]
 
+    @pl.when(has_off)
+    def _():
+        moduli_copy().start()
+
     spread[...] = jnp.zeros((128, 128), F32)
     for n in range(STEPS):
         spread[pl.ds(0, 64, stride=2), :] = probes[n] * (1.0 / (2.0 * DT))
@@ -245,11 +280,13 @@
 
     def over_planes(part, planes, cell, put):
         def body(i, packed):
-            cells = [(plane(part, i * planes + j), zb) for j in range(planes) for zb in range(4)]
-            values = [cell(x, zb) for x, zb in cells]
+            cells = [(plane(part, i * planes + j), zb, j) for j in range(planes) for zb in range(4)]
+            values = [cell(*where) for where in cells]
             packed = list(packed)
-            for (x, zb), value in zip(cells, values):
-                edge = put(x, zb, value)
+            for (x, zb, j), value in zip(cells, values):
+                edge = put(x, zb, value, j)
+                if edge is None:
+                    continue
                 k = x * 4 + zb
                 here = (lane >> 2) == k
                 for c in range(3):
@@ -261,7 +298,16 @@
         return lax.fori_loop(0, 4 // planes, body, (zero8,) * 3)
 
     def stress(cur, part, halos):
-        def cell(x, zb):
+        def d_x(c, x, zu, j):
+            if part != OFF:
+                return combine(U[cur, c, x, zu, :], U[cur, c, x + 1, zu, :],
+                               U[cur, c, x + 3, zu, :], U[cur, c, x + 4, zu, :])
+            ahead, second_ahead = U[cur, c, x + 2 + inward, zu, :], U[cur, c, x + 2 + 2 * inward, zu, :]
+            if j == 1:
+                ahead = ahead - U[cur, c, x + 2 - inward, zu, :]
+            return sign * (8.0 * ahead - second_ahead)
+
+        def cell(x, zb, j):
             z0 = zb * 8
             zs, zu = slice(z0, z0 + 8), slice(z0 + 8, z0 + 16)
             k = x * 4 + zb
@@ -270,8 +316,7 @@
             g = []
             for c in range(3):
                 f = U[cur, c, x + 2, zu, :]
-                dx = combine(U[cur, c, x, zu, :], U[cur, c, x + 1, zu, :],
-                             U[cur, c, x + 3, zu, :], U[cur, c, x + 4, zu, :])
+                dx = d_x(c, x, zu, j)
                 dr = combine(*[U[cur, c, x + 2, z0 + o:z0 + o + 8, :] for o in (6, 7, 9, 10)])
                 dy = combine(*shifted(f, pltpu.roll(halos[c], 126 - 4 * k, 1), lane))
                 g.append((dx + sx * dr, dy + sy * dr, st * dr))
@@ -280,17 +325,55 @@
             return (pressure + mu2 * g[0][0], mu * (g[0][1] + g[1][0]), mu * (g[0][2] + g[2][0]),
                     pressure + mu2 * g[1][1], mu * (g[1][2] + g[2][1]), pressure + mu2 * g[2][2])
 
-        def put(x, zb, value):
-            for j in range(6):
-                S[j, x + 2, zb * 8 + 8:zb * 8 + 16, :] = value[j]
+        def put(x, zb, value, j):
+            for i in range(6):
+                S[i, x + 2, zb * 8 + 8:zb * 8 + 16, :] = value[i]
+            if part == OFF:
+                for i in range(3):
+                    SA[i, x - 6 * turn, zb * 8:zb * 8 + 8, :] = value[i]
+                return None
             return value[1], value[3], value[4]
 
         return over_planes(part, 2, cell, put)
+
+    def added(first, near, j):
+        return first - 8.0 * near if j == 0 else near
+
+    def complete(cur):
+        def cell(x, zb, j):
+            zs, zu = slice(zb * 8, zb * 8 + 8), slice(zb * 8 + 8, zb * 8 + 16)
+            lam, mu = MET[3, x, zs, :], MET[4, x, zs, :]
+            at = outermost + 2 - inward
+            dx = [sign * added(U[cur, c, at - inward, zu, :], U[cur, c, at, zu, :], j) for c in range(3)]
+            side_pressure = lam * dx[0]
+            return (S[0, x + 2, zu, :] + (side_pressure + (mu + mu) * dx[0]), S[1, x + 2, zu, :] + mu * dx[1],
+                    S[2, x + 2, zu, :] + mu * dx[2], S[3, x + 2, zu, :] + side_pressure,
+                    S[5, x + 2, zu, :] + side_pressure, S[4, x + 2, zu, :])
+
+        def put(x, zb, value, j):
+            zu = slice(zb * 8 + 8, zb * 8 + 16)
+            for i, row in enumerate((0, 1, 2, 3, 5)):
+                S[row, x + 2, zu, :] = value[i]
+            return value[1], value[3], value[5]
+
+        return over_planes(OFF, 2, cell, put)
+
+    def complete_beyond(cur, parity):
+        for j in range(2):
+            at = 1 - turn if j == 0 else turn
+            for zb in range(4):
+                zs, zu = slice(zb * 8, zb * 8 + 8), slice(zb * 8 + 8, zb * 8 + 16)
+                lam, mu = MH[0, at, zs, :], MH[1, at, zs, :]
+                dx = [-sign * added(U[cur, c, second + 2, zu, :], U[cur, c, outermost + 2, zu, :], j)
+                      for c in range(3)]
+                scale = (lam + (mu + mu), mu, mu)
+                for c in range(3):
+                    S[c, outermost + 2 - (1 + j) * inward, zu, :] = AH[parity, c, at, zs, :] + scale[c] * dx[c]
 
     def forces(cur, part, halos):
         old = 1 - cur
 
-        def cell(x, zb):
+        def cell(x, zb, _):
             z0 = zb * 8
             zs, zu = slice(z0, z0 + 8), slice(z0 + 8, z0 + 16)
             k = x * 4 + zb
@@ -315,7 +398,7 @@
                 moved.append((fol, fol - p))
             return moved
 
-        def put(x, zb, value):
+        def put(x, zb, value, _):
             z0 = zb * 8
             for c in range(3):
                 U[old, c, x + 2, z0 + 8:z0 + 16, :] = value[c][0]
@@ -329,17 +412,25 @@
         more = n < STEPS - 1
         packed = stress(cur, INNER, y_wait(PU, HU, 0, INNER))
         y_send(packed, PS, HS, 1, INNER)
+        stress(cur, OFF, y_wait(PU, HU, 0, OFF))
+
+        @pl.when(has_off)
+        def _():
+            partial_copy(cur).start()
+
+        halos = y_wait(PU, HU, 0, ON)
+        u_wait(cur, ON)
+        packed = stress(cur, ON, halos)
+        s_copy().start()
+        y_send(packed, PS, HS, 1, ON)
 
         @pl.when(n > 0)
         def _():
             sketch(n - 1, True)
 
-        for part in (ON, OFF):
-            halos = y_wait(PU, HU, 0, part)
-            x_wait(u_planes(cur), 0, part)
-            packed = stress(cur, part, halos)
-            x_start(s_planes, 1, part)
-            y_send(packed, PS, HS, 1, part)
+        u_wait(cur, OFF)
+        packed = complete(cur)
+        y_send(packed, PS, HS, 1, OFF)
 
         packed = forces(cur, INNER, y_wait(PS, HS, 1, INNER))
 
@@ -350,12 +441,23 @@
         sketch(n, False)
         for part in (ON, OFF):
             halos = y_wait(PS, HS, 1, part)
-            x_wait(s_planes, 1, part)
+            if part == ON:
+                s_copy().wait()
+            else:
+                @pl.when(has_off)
+                def _():
+                    partial_copy(cur).wait()
+
+                @pl.when(has_off & (n == 0))
+                def _():
+                    moduli_copy().wait()
+
+                complete_beyond(cur, cur)
             packed = forces(cur, part, halos)
 
             @pl.when(more)
             def _():
-                x_start(u_planes(1 - cur), 0, part)
+                u_start(1 - cur, part)
                 y_send(packed, PU, HU, 0, part)
 
         return carry
@@ -445,9 +547,9 @@
         (3, 256, 128), (3, 256, 128), (2, 256, 128), (256, 128), (2, 256, 128), (256, 128), (STEPS, 64, 128),
         (128, 128), (2, 3, 12, ZP, 128), (6, 12, ZP, 128), (6, 8, 32, 128), (3, 8, 32, 128), (192, 128),
         (3, 3, 8, 128), (3, 3, 8, 128), (3, 2, 3, 8, 128), (3, 2, 3, 8, 128),
-        (8, 24, 128), (8, 24, 128), (16, 8, 128), (16, 8, 128), (8, 128), (16, 8, 128), (8, 128),
+        (3, 2, 32, 128), (2, 3, 2, 32, 128), (2, 2, 32, 128), (8, 24, 128), (8, 24, 128), (16, 8, 128), (16, 8, 128), (8, 128), (16, 8, 128), (8, 128),
     ]
-    sems = [(7,), (2, 2), (2, 2), (2, 3, 2), (2, 3, 2)] + [(8,)] * 2 + [(16,)] * 6
+    sems = [(7,), (4,), (4,), (), (), (2, 3, 2), (2, 3, 2), (2,), (2,), (2,)] + [(8,)] * 2 + [(16,)] * 6
     return pl.pallas_call(
         wave_kernel,
         name="wave",

time: 73 us -> 69.9 us (0.958)
  Pallas kernels: 72.3 us -> 69.1 us
    pallas_call x1, Pallas kernels: 66.9 us -> 63.7 us  [wave(): pl.pallas_call(wave_kernel, name='wave', out_shape=(jax.ShapeDtypeStruct(...]
where the time goes in v6:
time: 69.9 us; the launch traced here: 69.8 us
  Pallas kernels  69.1 us (99%)
    pallas_call x1, Pallas kernels, wave(): pl.pallas_call(wave_kernel, name='wave', out_shape=(jax.ShapeDtypeStruct(...  63.7 us
    pallas_call x1, Pallas kernels, finish(): pl.pallas_call(functools.partial(factor_kernel, scale), name='factor', ou...  5.42 us

profile of v6, /device:TPU:1, one launch (start us, length us, event | category | flops | bytes accessed | tf_op | source)
XLA Modules:
  0.0 69.8 jit_solution(3642925789938722753)
XLA Ops:
  0.6 63.7 %wave.1 = (f32[24,128]{1,0:T(8,128)S(1)}, f32[16,8,128]{2,1,0:T(8,128)S(1)}, f32[3,256,128]{2,1,0:T(8,128)S(1)}) custom-call(f32[3,256,128]{2,1,0:T(8,128)} %bitcast.8, f32[3,256,128]{2,1,0:T(8,128)} %bitcast.9, f32[2,256,128]{2,1,0:T(8,128)} %bitcast.10, f32[256,128]{1,0:T(8,128)} %bitcast.12, f32[2,256,128]{2,1,0:T(8,128)} %bitcast.11, ...), custom_call_target="tpu_custom_call" | custom-call | tf_op jit(solution)/shard_map/wave/pallas_call | solution.py:553
  64.3 5.4 %factor.1 = (f32[6,4,128]{2,1,0:T(4,128)}, f32[128,128]{1,0:T(8,128)}, f32[3,256,128]{2,1,0:T(8,128)}) custom-call(f32[16,8,128]{2,1,0:T(8,128)S(1)} %get-tuple-element.9.gram, f32[24,128]{1,0:T(8,128)S(1)} %get-tuple-element.10.tall, f32[3,256,128]{2,1,0:T(8,128)S(1)} %get-tuple-element.11.disp), custom_call_target="tpu_custom_call" | custom-call | tf_op jit(solution)/shard_map/factor/pallas_call | solution.py:628

commit v7 on v6

--- a/solution.py
+++ b/solution.py
@@ -439,6 +439,7 @@
             y_send(packed, PU, HU, 0, INNER)
 
         sketch(n, False)
+        moved = []
         for part in (ON, OFF):
             halos = y_wait(PS, HS, 1, part)
             if part == ON:
@@ -455,10 +456,13 @@
                 complete_beyond(cur, cur)
             packed = forces(cur, part, halos)
 
-            @pl.when(more)
-            def _():
+            moved.append(packed)
+
+        @pl.when(more)
+        def _():
+            for part in (OFF, ON):
+                y_send(moved[part - 1], PU, HU, 0, part)
                 u_start(1 - cur, part)
-                y_send(packed, PU, HU, 0, part)
 
         return carry
 
@@ -508,17 +512,23 @@
                 src_ref=src(peer), dst_ref=dst.at[slot], send_sem=send.at[peer], recv_sem=recv.at[slot],
                 device_id=dev(peer), device_id_type=MESH)
 
-        @pl.loop(0, 15)
+        @pl.loop(0, 15, unroll=5)
         def _(i):
             make(me, lax.rem(me + far_first(i, 8), 16)).start()
 
         def finish():
-            @pl.loop(1, 16)
+            @pl.loop(1, 16, unroll=5)
             def _(d):
                 peer = lax.rem(me + d, 16)
-                make(peer, peer).wait()
-
-        return finish
+                make(peer, peer).wait_recv()
+
+        def sent():
+            @pl.loop(1, 16, unroll=5)
+            def _(d):
+                peer = lax.rem(me + d, 16)
+                make(peer, peer).wait_send()
+
+        return finish, sent
 
     def summed(ref):
         parts = [ref[i] for i in range(16)]
@@ -526,19 +536,22 @@
             parts = [parts[i] + parts[i + 1] for i in range(0, len(parts), 2)]
         return parts[0]
 
-    finish = group(b_dev, b_me, lambda p: GL.at[p], RA, s1, r1)
+    finish, sent_a = group(b_dev, b_me, lambda p: GL.at[p], RA, s1, r1)
     RA[b_me] = GL[b_me]
     finish()
     part = summed(RA)
     PA[...] = part
-    finish = group(a_dev, a_me, lambda p: PA, RBB, s2, r2)
+    finish, sent_b = group(a_dev, a_me, lambda p: PA, RBB, s2, r2)
     RBB[a_me] = part
     finish()
     whole = summed(RBB)
     GS[...] = whole
-    finish = group(b_dev, b_me, lambda p: GS, gram, s3, r3)
+    finish, sent_c = group(b_dev, b_me, lambda p: GS, gram, s3, r3)
     gram[b_me] = whole
+    sent_a()
+    sent_b()
     finish()
+    sent_c()
 
 
 def wave(disp, vel, slopes, stretch, moduli, buoy, probes):

time: 69.9 us -> 69.5 us (level)
  no operation moved by 1% of the time
where the time goes in v7:
time: 69.5 us; the launch traced here: 69.4 us
  Pallas kernels  68.7 us (99%)
    pallas_call x1, Pallas kernels, wave(): pl.pallas_call(wave_kernel, name='wave', out_shape=(jax.ShapeDtypeStruct(...  63.3 us
    pallas_call x1, Pallas kernels, finish(): pl.pallas_call(functools.partial(factor_kernel, scale), name='factor', ou...  5.42 us

profile of v7, /device:TPU:1, one launch (start us, length us, event | category | flops | bytes accessed | tf_op | source)
XLA Modules:
  0.0 69.4 jit_solution(18229295802816060141)
XLA Ops:
  0.6 63.3 %wave.1 = (f32[24,128]{1,0:T(8,128)S(1)}, f32[16,8,128]{2,1,0:T(8,128)S(1)}, f32[3,256,128]{2,1,0:T(8,128)S(1)}) custom-call(f32[3,256,128]{2,1,0:T(8,128)} %bitcast.8, f32[3,256,128]{2,1,0:T(8,128)} %bitcast.9, f32[2,256,128]{2,1,0:T(8,128)} %bitcast.10, f32[256,128]{1,0:T(8,128)} %bitcast.12, f32[2,256,128]{2,1,0:T(8,128)} %bitcast.11, ...), custom_call_target="tpu_custom_call" | custom-call | tf_op jit(solution)/shard_map/wave/pallas_call | solution.py:566
  63.9 5.4 %factor.1 = (f32[6,4,128]{2,1,0:T(4,128)}, f32[128,128]{1,0:T(8,128)}, f32[3,256,128]{2,1,0:T(8,128)}) custom-call(f32[16,8,128]{2,1,0:T(8,128)S(1)} %get-tuple-element.9.gram, f32[24,128]{1,0:T(8,128)S(1)} %get-tuple-element.10.tall, f32[3,256,128]{2,1,0:T(8,128)S(1)} %get-tuple-element.11.disp), custom_call_target="tpu_custom_call" | custom-call | tf_op jit(solution)/shard_map/factor/pallas_call | solution.py:641

commit v8 on v7

--- a/solution.py
+++ b/solution.py
@@ -84,7 +84,7 @@
 
     barrier = pltpu.get_barrier_semaphore()
 
-    @pl.loop(0, 15)
+    @pl.loop(0, 15, unroll=5)
     def _(i):
         d = far_first(i, 8)
         pl.semaphore_signal(barrier, inc=1, device_id=a_dev(lax.rem(a_me + d, 16)), device_id_type=MESH)
@@ -477,7 +477,7 @@
             src_ref=PIECES.at[g], dst_ref=RB.at[slot], send_sem=s0.at[g], recv_sem=r0.at[slot],
             device_id=(gx, g), device_id_type=MESH)
 
-    @pl.loop(0, 7)
+    @pl.loop(0, 7, unroll=7)
     def _(i):
         piece(lax.rem(gy + far_first(i, 4), 8), gy).start()
 
@@ -491,7 +491,7 @@
             for c in range(3):
                 out[c, pl.ds(zb * 64 + x, 8, stride=8), :] = U[final, c, x + 2, zb * 8 + 8:zb * 8 + 16, :]
 
-    @pl.loop(1, 8)
+    @pl.loop(1, 8, unroll=7)
     def _(d):
         g = lax.rem(gy + d, 8)
         piece(g, g).wait()

time: 69.5 us -> 69.4 us (level)
  no operation moved by 1% of the time
where the time goes in v8:
time: 69.4 us; the launch traced here: 69.3 us
  Pallas kernels  68.7 us (99%)
    pallas_call x1, Pallas kernels, wave(): pl.pallas_call(wave_kernel, name='wave', out_shape=(jax.ShapeDtypeStruct(...  63.3 us
    pallas_call x1, Pallas kernels, finish(): pl.pallas_call(functools.partial(factor_kernel, scale), name='factor', ou...  5.42 us

profile of v8, /device:TPU:1, one launch (start us, length us, event | category | flops | bytes accessed | tf_op | source)
XLA Modules:
  0.0 69.3 jit_solution(6669098357417223986)
XLA Ops:
  0.6 63.3 %wave.1 = (f32[24,128]{1,0:T(8,128)S(1)}, f32[16,8,128]{2,1,0:T(8,128)S(1)}, f32[3,256,128]{2,1,0:T(8,128)S(1)}) custom-call(f32[3,256,128]{2,1,0:T(8,128)} %bitcast.8, f32[3,256,128]{2,1,0:T(8,128)} %bitcast.9, f32[2,256,128]{2,1,0:T(8,128)} %bitcast.10, f32[256,128]{1,0:T(8,128)} %bitcast.12, f32[2,256,128]{2,1,0:T(8,128)} %bitcast.11, ...), custom_call_target="tpu_custom_call" | custom-call | tf_op jit(solution)/shard_map/wave/pallas_call | solution.py:566
  63.9 5.4 %factor.1 = (f32[6,4,128]{2,1,0:T(4,128)}, f32[128,128]{1,0:T(8,128)}, f32[3,256,128]{2,1,0:T(8,128)}) custom-call(f32[16,8,128]{2,1,0:T(8,128)S(1)} %get-tuple-element.9.gram, f32[24,128]{1,0:T(8,128)S(1)} %get-tuple-element.10.tall, f32[3,256,128]{2,1,0:T(8,128)S(1)} %get-tuple-element.11.disp), custom_call_target="tpu_custom_call" | custom-call | tf_op jit(solution)/shard_map/factor/pallas_call | solution.py:641
